TPU v7x, 32 devices: a whole 2x2x4 slice. The times are simulated.
32 devices in a mesh: section: 2 (over core), dp: 16 (over z, y, x).
Axes of the slice: x: 2, y: 2, z: 4, core: 2. Of those that a mesh axis runs over, the one named last changes fastest.
Arguments:
- entry_pair: bfloat16 [2, 32, 256, 1024], P('section', 'dp'), may hold values from -6 to 6
- paragraph_labels: int32 [32, 256], P('dp'), may hold values from 0 to 1, never falling along the last dimension, each value on 1 to 192 neighbouring positions
- initial_norm_scaling: bfloat16 [2, 1024], P('section'), may hold values from 0.5 to 1.5
- initial_norm_offset: bfloat16 [2, 1024], P('section'), may hold values from -2 to 2
- log_fading_rates: bfloat16 [2, 1024], P('section'), may hold values from -8 to -2
- present_position_reward: bfloat16 [2, 1024], P('section'), may hold values from -1 to 1
- shift_ratio_lookup: bfloat16 [2, 1024], P('section'), may hold values from 0 to 1
- shift_ratio_content: bfloat16 [2, 1024], P('section'), may hold values from 0 to 1
- shift_ratio_accept: bfloat16 [2, 1024], P('section'), may hold values from 0 to 1
- attention_lookup_matrix: bfloat16 [2, 1024, 1024], P('section'), may hold values from -0.1875 to 0.1875
- attention_content_matrix: bfloat16 [2, 1024, 1024], P('section'), may hold values from -0.1875 to 0.1875
- attention_accept_matrix: bfloat16 [2, 1024, 1024], P('section'), may hold values from -0.1875 to 0.1875
- attention_exit_matrix: bfloat16 [2, 1024, 1024], P('section'), may hold values from -0.75 to 0.75
- latter_norm_scaling: bfloat16 [2, 1024], P('section'), may hold values from 0.5 to 1.5
- latter_norm_offset: bfloat16 [2, 1024], P('section'), may hold values from -2 to 2
- feedforward_lookup_ratio: bfloat16 [2, 1024], P('section'), may hold values from 0 to 1
- feedforward_accept_ratio: bfloat16 [2, 1024], P('section'), may hold values from 0 to 1
- feedforward_lookup_matrix: bfloat16 [2, 1024, 4096], P('section'), may hold values from -0.1875 to 0.1875
- feedforward_accept_matrix: bfloat16 [2, 1024, 1024], P('section'), may hold values from -0.1875 to 0.1875
- feedforward_content_matrix: bfloat16 [2, 4096, 1024], P('section'), may hold values from -0.09375 to 0.09375
Outputs:
- block_ends: float32 [2, 32, 256, 1024], P('section', 'dp')
- first_gain_gradient: float32 [2, 1024], P('section', 'dp')
- first_bias_gradient: float32 [2, 1024], P('section', 'dp')
- time_decay_gradient: float32 [2, 1024], P('section', 'dp')
- time_first_gradient: float32 [2, 1024], P('section', 'dp')
- blend_key_gradient: float32 [2, 1024], P('section', 'dp')
- blend_value_gradient: float32 [2, 1024], P('section', 'dp')
- blend_recept_gradient: float32 [2, 1024], P('section', 'dp')
- weight_key_gradient: float32 [2, 1024, 1024], P('section', 'dp')
- weight_value_gradient: float32 [2, 1024, 1024], P('section', 'dp')
- weight_recept_gradient: float32 [2, 1024, 1024], P('section', 'dp')
- weight_output_gradient: float32 [2, 1024, 1024], P('section', 'dp')
- second_gain_gradient: float32 [2, 1024], P('section', 'dp')
- second_bias_gradient: float32 [2, 1024], P('section', 'dp')
- channel_key_gradient: float32 [2, 1024], P('section', 'dp')
- channel_recept_gradient: float32 [2, 1024], P('section', 'dp')
- hidden_key_gradient: float32 [2, 1024, 4096], P('section', 'dp')
- hidden_recept_gradient: float32 [2, 1024, 1024], P('section', 'dp')
- hidden_value_gradient: float32 [2, 4096, 1024], P('section', 'dp')
Inputs may be any that keep to these rules, and one draw needn't show every extreme that they name: `paragraph_labels`: in every row the document number is 0 up to some token and 1 from there on, so a row holds two documents, each of 64 to 192 tokens.
All inputs are finite; a program needn't handle non-finite values.
Results may differ from a plain program's by a relative error of at most 0.015.
Values may be sent and summed in bfloat16 or wider, within the bound.
No kernel may reach another device: no remote copies, remote signals or barrier semaphores. Data moves between devices by JAX's collectives and lax.ppermute only.
A program may use at most 256 MiB of HBM per device.

v0:
```python
import jax
import jax.numpy as jnp
from jax import lax
from jax.sharding import PartitionSpec as P

BLOCK = 16


def from_behind(block, axis, distance):
    devices = range(lax.axis_size(axis))
    route = [(i - distance, i) for i in devices if i - distance in devices]
    return lax.ppermute(block, axis, route)


def norm_rows(values, norm_gain, norm_bias):
    average = jnp.mean(values, axis=-1, keepdims=True)
    centered = values - average
    variance = jnp.mean(centered * centered, axis=-1, keepdims=True)
    return centered * lax.rsqrt(variance + 1e-05) * norm_gain + norm_bias


def previous(values, concatenated_texts):
    before = jnp.concatenate([jnp.zeros_like(values[:1]), values[:-1]], axis=0)
    joined = jnp.concatenate(
        [jnp.zeros((1,), jnp.bool_), concatenated_texts[1:] == concatenated_texts[:-1]]
    )
    return jnp.where(joined[:, None], before, jnp.zeros_like(before))


def blend(normed, shifted_in, factor):
    return normed * factor + shifted_in * (1.0 - factor)


def scaled_lookups(
    lookup_projected,
    content_projected,
    log_fading_rates,
    present_position_reward,
    concatenated_texts,
):
    decay_rate = jnp.exp(log_fading_rates)
    offsets = jnp.arange(BLOCK, dtype=jnp.float32)
    distance = offsets[:, None] - offsets[None, :] - 1.0
    causal = distance >= 0

    def mix_block(carry, piece):
        dividend_memory, divisor_memory, last_doc = carry
        lookup_block_piece, content_block_piece, doc_block = piece
        visible = (doc_block[:, None] == doc_block[None, :]) & causal
        exponent = -distance[:, :, None] * decay_rate + lookup_block_piece[None, :, :]
        linear_attention_routine = jnp.where(visible[:, :, None], jnp.exp(exponent), 0.0)
        running_memory = jnp.where(
            (doc_block == last_doc)[:, None], jnp.exp(-offsets[:, None] * decay_rate), 0.0
        )
        extra_reward_increment = jnp.exp(present_position_reward + lookup_block_piece)
        dividend_total = (
            running_memory * dividend_memory
            + jnp.sum(linear_attention_routine * content_block_piece[None, :, :], axis=1)
            + extra_reward_increment * content_block_piece
        )
        divisor_total = (
            running_memory * divisor_memory
            + jnp.sum(linear_attention_routine, axis=1)
            + extra_reward_increment
        )
        tail_doc = doc_block[BLOCK - 1]
        tail_kernel = jnp.where(
            (doc_block == tail_doc)[:, None],
            jnp.exp(-(BLOCK - 1.0 - offsets)[:, None] * decay_rate + lookup_block_piece),
            0.0,
        )
        keep_old = jnp.where(tail_doc == last_doc, jnp.exp(-BLOCK * decay_rate), 0.0)
        top_next = keep_old * dividend_memory + jnp.sum(tail_kernel * content_block_piece, axis=0)
        bottom_next = keep_old * divisor_memory + jnp.sum(tail_kernel, axis=0)
        return ((top_next, bottom_next, tail_doc), dividend_total / divisor_total)

    width = lookup_projected.shape[1]
    blocks = lookup_projected.shape[0] // BLOCK
    start = (
        jnp.zeros((width,), jnp.float32),
        jnp.zeros((width,), jnp.float32),
        jnp.array(-1, jnp.int32),
    )
    pieces = (
        lookup_projected.reshape(blocks, BLOCK, width),
        content_projected.reshape(blocks, BLOCK, width),
        concatenated_texts.reshape(blocks, BLOCK),
    )
    _, outputs = lax.scan(jax.checkpoint(mix_block), start, pieces)
    return outputs.reshape(lookup_projected.shape)


def time_inputs(
    values, norm_gain, norm_bias, key_factor, value_factor, recept_factor, concatenated_texts
):
    normed = norm_rows(values, norm_gain, norm_bias)
    shifted_in = previous(normed, concatenated_texts)
    return (
        blend(normed, shifted_in, key_factor),
        blend(normed, shifted_in, value_factor),
        blend(normed, shifted_in, recept_factor),
    )


def channel_inputs(middle, norm_gain, norm_bias, key_factor, recept_factor, concatenated_texts):
    normed = norm_rows(middle, norm_gain, norm_bias)
    shifted_in = previous(normed, concatenated_texts)
    return (blend(normed, shifted_in, key_factor), blend(normed, shifted_in, recept_factor))


def attention_result(
    lookup_projected,
    content_projected,
    accept_logits,
    log_fading_rates,
    present_position_reward,
    concatenated_texts,
):
    return jax.nn.sigmoid(accept_logits) * scaled_lookups(
        lookup_projected,
        content_projected,
        log_fading_rates,
        present_position_reward,
        concatenated_texts,
    )


def product(left, right):
    return jnp.dot(left, right, preferred_element_type=jnp.float32)


def outer_product(left, right):
    return lax.dot_general(
        left, right, (((0,), (0,)), ((), ())), preferred_element_type=jnp.float32
    )


def back_product(deltas, right):
    return lax.dot_general(
        deltas, right, (((1,), (1,)), ((), ())), preferred_element_type=jnp.float32
    )


def forward_layer(block_in, concatenated_texts, learned_parameters):
    (
        initial_norm_scaling,
        initial_norm_offset,
        log_fading_rates,
        present_position_reward,
        shift_ratio_lookup,
        shift_ratio_content,
        shift_ratio_accept,
        attention_lookup_matrix,
        attention_content_matrix,
        attention_accept_matrix,
        attention_exit_matrix,
        latter_norm_scaling,
        latter_norm_offset,
        feedforward_lookup_ratio,
        feedforward_accept_ratio,
        feedforward_lookup_matrix,
        feedforward_accept_matrix,
        feedforward_content_matrix,
    ) = learned_parameters
    state_in = block_in.astype(jnp.float32)
    key_in, value_in, recept_in = (
        element_entry.astype(jnp.bfloat16)
        for element_entry in time_inputs(
            state_in,
            initial_norm_scaling,
            initial_norm_offset,
            shift_ratio_lookup,
            shift_ratio_content,
            shift_ratio_accept,
            concatenated_texts,
        )
    )
    lookup_projected = product(key_in, attention_lookup_matrix)
    content_projected = product(value_in, attention_content_matrix)
    accept_logits = product(recept_in, attention_accept_matrix)
    combined_input = attention_result(
        lookup_projected,
        content_projected,
        accept_logits,
        log_fading_rates,
        present_position_reward,
        concatenated_texts,
    ).astype(jnp.bfloat16)
    middle = state_in + product(combined_input, attention_exit_matrix)
    hidden_in, gate_in = (
        element_entry.astype(jnp.bfloat16)
        for element_entry in channel_inputs(
            middle,
            latter_norm_scaling,
            latter_norm_offset,
            feedforward_lookup_ratio,
            feedforward_accept_ratio,
            concatenated_texts,
        )
    )
    hidden_pre = product(hidden_in, feedforward_lookup_matrix)
    hidden_act = jnp.square(jax.nn.relu(hidden_pre)).astype(jnp.bfloat16)
    hidden_out = product(hidden_act, feedforward_content_matrix)
    gate_pre = product(gate_in, feedforward_accept_matrix)
    result = middle + jax.nn.sigmoid(gate_pre) * hidden_out
    kept = (
        state_in,
        key_in,
        value_in,
        recept_in,
        lookup_projected,
        content_projected,
        accept_logits,
        combined_input,
        middle,
        hidden_in,
        gate_in,
        hidden_pre,
        hidden_out,
        gate_pre,
    )
    return (result.astype(jnp.bfloat16), kept)


def backward_channel(incoming, concatenated_texts, learned_parameters, kept):
    (
        initial_norm_scaling,
        initial_norm_offset,
        log_fading_rates,
        present_position_reward,
        shift_ratio_lookup,
        shift_ratio_content,
        shift_ratio_accept,
        attention_lookup_matrix,
        attention_content_matrix,
        attention_accept_matrix,
        attention_exit_matrix,
        latter_norm_scaling,
        latter_norm_offset,
        feedforward_lookup_ratio,
        feedforward_accept_ratio,
        feedforward_lookup_matrix,
        feedforward_accept_matrix,
        feedforward_content_matrix,
    ) = learned_parameters
    (
        state_in,
        key_in,
        value_in,
        recept_in,
        lookup_projected,
        content_projected,
        accept_logits,
        combined_input,
        middle,
        hidden_in,
        gate_in,
        hidden_pre,
        hidden_out,
        gate_pre,
    ) = kept
    gate_sig = jax.nn.sigmoid(gate_pre)
    delta_out = (incoming * gate_sig).astype(jnp.bfloat16)
    delta_gate = (incoming * hidden_out * gate_sig * (1.0 - gate_sig)).astype(jnp.bfloat16)
    hidden_act = jnp.square(jax.nn.relu(hidden_pre)).astype(jnp.bfloat16)
    hidden_value_change = outer_product(hidden_act, delta_out)
    delta_act = back_product(delta_out, feedforward_content_matrix)
    delta_pre = (delta_act * 2.0 * jax.nn.relu(hidden_pre)).astype(jnp.bfloat16)
    hidden_key_change = outer_product(hidden_in, delta_pre)
    hidden_recept_change = outer_product(gate_in, delta_gate)
    _, pull_channel = jax.vjp(
        lambda middle_in, norm_gain, norm_bias, key_factor, recept_factor: channel_inputs(
            middle_in, norm_gain, norm_bias, key_factor, recept_factor, concatenated_texts
        ),
        middle,
        latter_norm_scaling,
        latter_norm_offset,
        feedforward_lookup_ratio,
        feedforward_accept_ratio,
    )
    (
        middle_back,
        second_gain_change,
        second_bias_change,
        channel_key_change,
        channel_recept_change,
    ) = pull_channel(
        (
            back_product(delta_pre, feedforward_lookup_matrix),
            back_product(delta_gate, feedforward_accept_matrix),
        )
    )
    middle_delta = incoming + middle_back
    changes = (
        second_gain_change,
        second_bias_change,
        channel_key_change,
        channel_recept_change,
        hidden_key_change,
        hidden_recept_change,
        hidden_value_change,
    )
    return (middle_delta, changes)


def backward_time(middle_delta, concatenated_texts, learned_parameters, kept):
    (
        initial_norm_scaling,
        initial_norm_offset,
        log_fading_rates,
        present_position_reward,
        shift_ratio_lookup,
        shift_ratio_content,
        shift_ratio_accept,
        attention_lookup_matrix,
        attention_content_matrix,
        attention_accept_matrix,
        attention_exit_matrix,
        latter_norm_scaling,
        latter_norm_offset,
        feedforward_lookup_ratio,
        feedforward_accept_ratio,
        feedforward_lookup_matrix,
        feedforward_accept_matrix,
        feedforward_content_matrix,
    ) = learned_parameters
    (
        state_in,
        key_in,
        value_in,
        recept_in,
        lookup_projected,
        content_projected,
        accept_logits,
        combined_input,
        middle,
        hidden_in,
        gate_in,
        hidden_pre,
        hidden_out,
        gate_pre,
    ) = kept
    delta_branch = middle_delta.astype(jnp.bfloat16)
    weight_output_change = outer_product(combined_input, delta_branch)
    delta_mixed = back_product(delta_branch, attention_exit_matrix)
    _, pull_time = jax.vjp(
        lambda lookup_argument, content_argument, accept_argument, fading_argument, extra_reward_argument: attention_result(
            lookup_argument,
            content_argument,
            accept_argument,
            fading_argument,
            extra_reward_argument,
            concatenated_texts,
        ),
        lookup_projected,
        content_projected,
        accept_logits,
        log_fading_rates,
        present_position_reward,
    )
    delta_key, delta_value, delta_recept, time_decay_change, time_first_change = pull_time(
        delta_mixed
    )
    delta_key = delta_key.astype(jnp.bfloat16)
    delta_value = delta_value.astype(jnp.bfloat16)
    delta_recept = delta_recept.astype(jnp.bfloat16)
    weight_key_change = outer_product(key_in, delta_key)
    weight_value_change = outer_product(value_in, delta_value)
    weight_recept_change = outer_product(recept_in, delta_recept)
    _, pull_norm = jax.vjp(
        lambda state_arg, norm_gain, norm_bias, key_factor, value_factor, recept_factor: time_inputs(
            state_arg,
            norm_gain,
            norm_bias,
            key_factor,
            value_factor,
            recept_factor,
            concatenated_texts,
        ),
        state_in,
        initial_norm_scaling,
        initial_norm_offset,
        shift_ratio_lookup,
        shift_ratio_content,
        shift_ratio_accept,
    )
    (
        state_back,
        first_gain_change,
        first_bias_change,
        blend_key_change,
        blend_value_change,
        blend_recept_change,
    ) = pull_norm(
        (
            back_product(delta_key, attention_lookup_matrix),
            back_product(delta_value, attention_content_matrix),
            back_product(delta_recept, attention_accept_matrix),
        )
    )
    changes = (
        first_gain_change,
        first_bias_change,
        time_decay_change,
        time_first_change,
        blend_key_change,
        blend_value_change,
        blend_recept_change,
        weight_key_change,
        weight_value_change,
        weight_recept_change,
        weight_output_change,
    )
    return (middle_delta + state_back, changes)


def local(
    entry_pair,
    paragraph_labels,
    initial_norm_scaling,
    initial_norm_offset,
    log_fading_rates,
    present_position_reward,
    shift_ratio_lookup,
    shift_ratio_content,
    shift_ratio_accept,
    attention_lookup_matrix,
    attention_content_matrix,
    attention_accept_matrix,
    attention_exit_matrix,
    latter_norm_scaling,
    latter_norm_offset,
    feedforward_lookup_ratio,
    feedforward_accept_ratio,
    feedforward_lookup_matrix,
    feedforward_accept_matrix,
    feedforward_content_matrix,
):
    section_count = lax.axis_size("section")
    section_rank = lax.axis_index("section")
    micro_count = paragraph_labels.shape[0]
    own_rows = entry_pair[0]
    learned_parameters = tuple(
        (
            element_entry[0].astype(jnp.float32) if element_entry.ndim == 2 else element_entry[0]
            for element_entry in (
                initial_norm_scaling,
                initial_norm_offset,
                log_fading_rates,
                present_position_reward,
                shift_ratio_lookup,
                shift_ratio_content,
                shift_ratio_accept,
                attention_lookup_matrix,
                attention_content_matrix,
                attention_accept_matrix,
                attention_exit_matrix,
                latter_norm_scaling,
                latter_norm_offset,
                feedforward_lookup_ratio,
                feedforward_accept_ratio,
                feedforward_lookup_matrix,
                feedforward_accept_matrix,
                feedforward_content_matrix,
            )
        )
    )
    step_count = micro_count + section_count - 1
    received = jnp.zeros(own_rows.shape[1:], jnp.bfloat16)
    block_ends = jnp.zeros(own_rows.shape, jnp.float32)
    kept_steps = []
    for step_index in range(step_count):
        batch_index = step_index - section_rank
        active = (batch_index >= 0) & (batch_index < micro_count)
        row_index = jnp.clip(batch_index, 0, micro_count - 1)
        concatenated_texts = lax.dynamic_index_in_dim(
            paragraph_labels, row_index, 0, keepdims=False
        )
        own_row = lax.dynamic_index_in_dim(own_rows, row_index, 0, keepdims=False)
        block_in = jnp.where(section_rank == 0, own_row, received)
        result, kept = forward_layer(block_in, concatenated_texts, learned_parameters)
        kept_steps.append(kept)
        placed = lax.dynamic_update_index_in_dim(
            block_ends, result.astype(jnp.float32), row_index, 0
        )
        block_ends = jnp.where(active & (section_rank == section_count - 1), placed, block_ends)
        if step_index + 1 < step_count:
            received = from_behind(result, "section", 1)
    received = jnp.zeros(own_rows.shape[1:], jnp.bfloat16)
    time_totals = None
    channel_totals = None
    for step_index in range(step_count):
        batch_index = step_index - (section_count - 1 - section_rank)
        active = (batch_index >= 0) & (batch_index < micro_count)
        row_index = jnp.clip(batch_index, 0, micro_count - 1)
        concatenated_texts = lax.dynamic_index_in_dim(
            paragraph_labels, row_index, 0, keepdims=False
        )
        own_row = lax.dynamic_index_in_dim(own_rows, row_index, 0, keepdims=False)
        kept = kept_steps[min(max(step_index - section_count + 1, 0), step_count - 1)]
        candidate = kept_steps[min(max(step_index - section_count + 1 + 2, 0), step_count - 1)]
        kept = jax.tree.map(
            lambda here, there: jnp.where(section_rank == 1, there, here), kept, candidate
        )
        incoming = jnp.where(section_rank == section_count - 1, own_row, received).astype(
            jnp.float32
        )
        middle_delta, channel_changes = backward_channel(
            incoming, concatenated_texts, learned_parameters, kept
        )
        channel_changes = tuple(
            (jnp.where(active, element_entry, 0.0) for element_entry in channel_changes)
        )
        if channel_totals is None:
            channel_totals = channel_changes
        else:
            channel_totals = tuple(
                (left + right for left, right in zip(channel_totals, channel_changes))
            )
        state_delta, time_changes = backward_time(
            middle_delta, concatenated_texts, learned_parameters, kept
        )
        time_changes = tuple(
            (jnp.where(active, element_entry, 0.0) for element_entry in time_changes)
        )
        if time_totals is None:
            time_totals = time_changes
        else:
            time_totals = tuple((left + right for left, right in zip(time_totals, time_changes)))
        placed = lax.dynamic_update_index_in_dim(block_ends, state_delta, row_index, 0)
        block_ends = jnp.where(active & (section_rank == 0), placed, block_ends)
        if step_index + 1 < step_count:
            received = from_behind(state_delta.astype(jnp.bfloat16), "section", -1)
    totals = time_totals + channel_totals
    summed = (
        lax.psum_scatter(totals[0], "dp", scatter_dimension=0, tiled=True),
        lax.psum_scatter(totals[1], "dp", scatter_dimension=0, tiled=True),
        lax.psum_scatter(totals[2], "dp", scatter_dimension=0, tiled=True),
        lax.psum_scatter(totals[3], "dp", scatter_dimension=0, tiled=True),
        lax.psum_scatter(totals[4], "dp", scatter_dimension=0, tiled=True),
        lax.psum_scatter(totals[5], "dp", scatter_dimension=0, tiled=True),
        lax.psum_scatter(totals[6], "dp", scatter_dimension=0, tiled=True),
        lax.psum_scatter(totals[7], "dp", scatter_dimension=0, tiled=True),
        lax.psum_scatter(totals[8], "dp", scatter_dimension=0, tiled=True),
        lax.psum_scatter(totals[9], "dp", scatter_dimension=0, tiled=True),
        lax.psum_scatter(totals[10], "dp", scatter_dimension=0, tiled=True),
        lax.psum_scatter(totals[11], "dp", scatter_dimension=0, tiled=True),
        lax.psum_scatter(totals[12], "dp", scatter_dimension=0, tiled=True),
        lax.psum_scatter(totals[13], "dp", scatter_dimension=0, tiled=True),
        lax.psum_scatter(totals[14], "dp", scatter_dimension=0, tiled=True),
        lax.psum_scatter(totals[15], "dp", scatter_dimension=0, tiled=True),
        lax.psum_scatter(totals[16], "dp", scatter_dimension=0, tiled=True),
        lax.psum_scatter(totals[17], "dp", scatter_dimension=0, tiled=True),
    )
    return (block_ends[None],) + tuple((element_entry[None] for element_entry in summed))


def solution(mesh):
    in_specs = (
        P("section", "dp", None, None),
        P("dp", None),
        P("section", None),
        P("section", None),
        P("section", None),
        P("section", None),
        P("section", None),
        P("section", None),
        P("section", None),
        P("section", None, None),
        P("section", None, None),
        P("section", None, None),
        P("section", None, None),
        P("section", None),
        P("section", None),
        P("section", None),
        P("section", None),
        P("section", None, None),
        P("section", None, None),
        P("section", None, None),
    )
    out_specs = (
        P("section", "dp", None, None),
        P("section", "dp"),
        P("section", "dp"),
        P("section", "dp"),
        P("section", "dp"),
        P("section", "dp"),
        P("section", "dp"),
        P("section", "dp"),
        P("section", "dp", None),
        P("section", "dp", None),
        P("section", "dp", None),
        P("section", "dp", None),
        P("section", "dp"),
        P("section", "dp"),
        P("section", "dp"),
        P("section", "dp"),
        P("section", "dp", None),
        P("section", "dp", None),
        P("section", "dp", None),
    )
    return jax.shard_map(local, mesh=mesh, in_specs=in_specs, out_specs=out_specs, check_vma=False)
```

profile of v0, /device:TPU:0, one launch (start us, length us, event | category | flops | bytes accessed | tf_op | source)
XLA Modules:
  0.0 2836.0 jit_solution(12404204426290660514)
XLA Ops:
  35.4 98.1 %while.213 = (s32[]{:T(128)}, f32[1024]{0:T(1024)S(1)}, f32[1024]{0:T(1024)S(1)}, s32[]{:T(128)}, f32[16,16,1024]{2,1,0:T(8,128)}, /*index=5*/s32[16,16]{1,0:T(8...) while((s32[]{:T(128)}, f32[1024]{0:T(1024)S(1)}, ...), condition=%wide.region_7.8_spmd.clone, body=%wide.region_2.7_spmd.clone.sunk | while | flops 1826900 | bytes 924917 | solution.py:89
  184.0 98.1 %while.214 = (s32[]{:T(128)}, f32[1024]{0:T(1024)S(1)}, f32[1024]{0:T(1024)S(1)}, s32[]{:T(128)}, f32[16,16,1024]{2,1,0:T(8,128)}, /*index=5*/s32[16,16]{1,0:T(8...) while((s32[]{:T(128)}, f32[1024]{0:T(1024)S(1)}, ...), condition=%wide.region_17.18_spmd.clone, body=%wide.region_12.17_spmd.clone.sunk | while | flops 1826900 | bytes 924917 | solution.py:89
  303.1 8.8 fusion.326
  327.7 172.7 %while.219 = (s32[]{:T(128)}, f32[1024]{0:T(1024)S(1)}, f32[1024]{0:T(1024)S(1)}, s32[]{:T(128)}, f32[16,16,1024]{2,1,0:T(8,128)}, /*index=5*/f32[16,1024]{1,0:T...) while((s32[]{:T(128)}, f32[1024]{0:T(1024)S(1)}, ...), condition=%wide.region_39.40_spmd.clone.clone.clone, body=%wide.region_34.39_spmd.clone.clone.clone.sunk | while | flops 1825060 | bytes 940225 | solution.py:89
  509.2 237.9 %while.216 = (s32[]{:T(128)}, f32[1024]{0:T(1024)}, f32[1024]{0:T(1024)}, f32[1024]{0:T(1024)}, f32[1024]{0:T(1024)}, /*index=5*/bf16[16,16,1024]{2,1,0:T(8,128)...) while((s32[]{:T(128)}, f32[1024]{0:T(1024)}, ...), condition=%wide.region_51.52_spmd.clone, body=%wide.region_40.51_spmd.clone.sunk | while | flops 5538901 | bytes 2348647 | solution.py:89
  772.0 109.4 %while.215 = (s32[]{:T(128)}, f32[1024]{0:T(1024)S(1)}, f32[1024]{0:T(1024)S(1)}, s32[]{:T(128)}, f32[16,16,1024]{2,1,0:T(8,128)}, /*index=5*/s32[16,16]{1,0:T(8...) while((s32[]{:T(128)}, f32[1024]{0:T(1024)S(1)}, ...), condition=%wide.region_27.28_spmd.clone, body=%wide.region_22.27_spmd.clone.sunk | while | flops 1826900 | bytes 924917 | solution.py:89
  900.9 169.5 %while.220 = (s32[]{:T(128)}, f32[1024]{0:T(1024)S(1)}, f32[1024]{0:T(1024)S(1)}, s32[]{:T(128)}, f32[16,16,1024]{2,1,0:T(8,128)}, /*index=5*/f32[16,1024]{1,0:T...) while((s32[]{:T(128)}, f32[1024]{0:T(1024)S(1)}, ...), condition=%wide.region_65.66_spmd.clone.clone.clone, body=%wide.region_60.65_spmd.clone.clone.clone.sunk | while | flops 1825060 | bytes 940225 | solution.py:89
  1073.1 115.7 %while.221 = (s32[]{:T(128)}, f32[1024]{0:T(1024)S(1)}, f32[1024]{0:T(1024)S(1)}, s32[]{:T(128)}, f32[16,16,1024]{2,1,0:T(8,128)}, /*index=5*/f32[16,1024]{1,0:T...) while((s32[]{:T(128)}, f32[1024]{0:T(1024)S(1)}, ...), condition=%wide.region_91.92_spmd.clone.clone.clone, body=%wide.region_86.91_spmd.clone.clone.clone.sunk | while | flops 1825060 | bytes 940225 | solution.py:89
  1189.0 8.9 fusion.325
  1226.6 205.9 %while.217 = (s32[]{:T(128)}, f32[1024]{0:T(1024)S(1)}, f32[1024]{0:T(1024)S(1)}, f32[1024]{0:T(1024)}, f32[1024]{0:T(1024)}, /*index=5*/bf16[16,16,1024]{2,1,0:...) while((s32[]{:T(128)}, f32[1024]{0:T(1024)S(1)}, ...), condition=%wide.region_77.78_spmd.clone, body=%wide.region_66.77_spmd.clone.sunk | while | flops 5538901 | bytes 2348647 | solution.py:89
  1451.7 7.7 fusion.201
  1473.9 153.1 %while.218 = (s32[]{:T(128)}, f32[1024]{0:T(1024)S(1)}, f32[1024]{0:T(1024)S(1)}, f32[1024]{0:T(1024)S(1)}, f32[1024]{0:T(1024)S(1)}, /*index=5*/bf16[16,16,1024...) while((s32[]{:T(128)}, f32[1024]{0:T(1024)S(1)}, ...), condition=%wide.region_103.104_spmd.clone, body=%wide.region_92.103_spmd.clone.sunk | while | flops 5538901 | bytes 2346275 | solution.py:89
  1660.1 9.9 fusion.349
  1670.0 8.1 fusion.347
  1678.1 11.8 select_add_fusion.7
  1691.1 11.3 fusion.204
  1702.4 8.5 fusion.205
  1710.9 13.0 select_add_fusion.6
  1748.5 79.3 %all-reduce.29 = (f32[1024]{0:T(1024)S(1)}, f32[1024]{0:T(1024)S(1)}, f32[1024]{0:T(1024)S(1)}, f32[1024]{0:T(1024)S(1)}, f32[1024]{0:T(1024)S(1)}, /*index=5*/f...) all-reduce(f32[1024]{0:T(1024)S(1)} %select_add_fusion.23, ...), channel_id=2, replica_groups=mesh['section'=2,'dp'=16] {'dp'}, use_global_device_ids=true, to_apply=%region_111.112.clone | all-reduce | flops 11264 | bytes 90112
  1837.4 92.8 %reduce-scatter.12.cloned.1.call-done = f32[64,1024]{1,0:T(8,128)} async-done(((f32[1024,1024]{1,0:T(8,128)}), f32[64,1024]{1,0:T(8,128)}) %reduce-scatter.12.cloned.1.call-update) | async-done | bytes 262160 | tf_op jit(solution)/shard_map/reduce_scatter | solution.py:545
  1930.2 97.5 %reduce-scatter.14.cloned.1.call-done = f32[64,1024]{1,0:T(8,128)} async-done(((f32[1024,1024]{1,0:T(8,128)}), f32[64,1024]{1,0:T(8,128)}) %reduce-scatter.14.cloned.1.call-update) | async-done | bytes 262160 | tf_op jit(solution)/shard_map/reduce_scatter | solution.py:546
  2027.7 97.5 %reduce-scatter.18.cloned.1.call-done = f32[64,1024]{1,0:T(8,128)} async-done(((f32[1024,1024]{1,0:T(8,128)}), f32[64,1024]{1,0:T(8,128)}) %reduce-scatter.18.cloned.1.call-update) | async-done | bytes 262160 | tf_op jit(solution)/shard_map/reduce_scatter | solution.py:552
  2125.2 348.7 %reduce-scatter.16.cloned.1.call-done = f32[64,4096]{1,0:T(8,128)} async-done(((f32[1024,4096]{1,0:T(8,128)}), f32[64,4096]{1,0:T(8,128)}) %reduce-scatter.16.cloned.1.call-update) | async-done | bytes 1048592 | tf_op jit(solution)/shard_map/reduce_scatter | solution.py:551
  2473.9 354.9 %reduce-scatter.20.cloned.1.call-done = f32[256,1024]{1,0:T(8,128)} async-done(((f32[4096,1024]{1,0:T(8,128)}), f32[256,1024]{1,0:T(8,128)}) %reduce-scatter.20.cloned.1.call-update) | async-done | bytes 1048592 | tf_op jit(solution)/shard_map/reduce_scatter | solution.py:553
  (3048 shorter events, 1460.3 us)
Async XLA Ops:
  7.2 130.1 %copy-start = (bf16[1,1024,1024]{2,1,0:T(8,128)(2,1)S(1)}, bf16[1,1024,1024]{2,1,0:T(8,128)(2,1)}, u32[]{:S(2)}) copy-start(bf16[1,1024,1024]{2,1,0:T(8,128)(2,1)} %param.50) | copy-start | bytes 6291460
  7.2 1830.2 %reduce-scatter.8.cloned.1.call-start = ((), (), s32[]{:S(2)}) async-start(), calls=%async_computation.7 | async-start | bytes 4456448 | tf_op jit(solution)/shard_map/reduce_scatter | solution.py:543
  28.2 139.5 %copy-start.238 = (pred[256]{0:T(512)(128)(4,1)}, pred[256]{0:T(512)(128)(4,1)S(1)}, u32[]{:S(2)}) copy-start(pred[256]{0:T(512)(128)(4,1)S(1)} %get-tuple-element.3690) | copy-start | bytes 772
  34.3 99.2 %copy-start.236 = (bf16[1,1024]{1,0:T(2,128)(2,1)S(1)}, bf16[1,1024]{1,0:T(2,128)(2,1)}, u32[]{:S(2)}) copy-start(bf16[1,1024]{1,0:T(2,128)(2,1)} %param.52) | copy-start | bytes 6148
  34.3 99.2 %copy-start.237 = (bf16[1,1024]{1,0:T(2,128)(2,1)S(1)}, bf16[1,1024]{1,0:T(2,128)(2,1)}, u32[]{:S(2)}) copy-start(bf16[1,1024]{1,0:T(2,128)(2,1)} %param.51) | copy-start | bytes 6148
  155.8 15.9 collective-permute-start
  167.7 154.2 %copy-start.248 = (pred[255]{0:T(512)(128)(4,1)}, pred[255]{0:T(512)(128)(4,1)S(1)}, u32[]{:S(2)}) copy-start(pred[255]{0:T(512)(128)(4,1)S(1)} %slice.207) | copy-start | bytes 769
  287.8 34.4 %copy-start.55 = (f32[256,1024]{1,0:T(8,128)}, f32[256,1024]{1,0:T(8,128)S(1)}, u32[]{:S(2)}) copy-start(f32[256,1024]{1,0:T(8,128)S(1)} %get-tuple-element.3561) | copy-start | bytes 3145732
  295.6 206.9 %copy-start.219 = (f32[256]{0:T(256)}, f32[256]{0:T(256)S(1)}, u32[]{:S(2)}) copy-start(f32[256]{0:T(256)S(1)} %broadcast_multiply_fusion.4) | copy-start | bytes 3076
  311.9 190.6 %collective-permute-start.1 = (bf16[256,1024]{1,0:T(8,128)(2,1)}, bf16[256,1024]{1,0:T(8,128)(2,1)}, u32[]{:S(2)}, u32[]{:S(2)}) collective-permute-start(bf16[256,1024]{1,0:T(8,128)(2,1)} %get-tuple-element.3563), channel_id=1, source_target_pairs={{0,16},{1,17},{2,18},{3,19},{4,20},{5,21},{6,22},{7,23},{8,24},{9,... | collective-permute-start | bytes 1572872 | tf_op jit(solution)/shard_map/ppermute | solution.py:12
  896.7 304.9 %collective-permute-start.2 = (bf16[256,1024]{1,0:T(8,128)(2,1)}, bf16[256,1024]{1,0:T(8,128)(2,1)}, u32[]{:S(2)}, u32[]{:S(2)}) collective-permute-start(bf16[256,1024]{1,0:T(8,128)(2,1)} %fusion.417), channel_id=1, source_target_pairs={{16,0},{17,1},{18,2},{19,3},{20,4},{21,5},{22,6},{23,7},{24,8},{25... | collective-permute-start | bytes 1572872 | tf_op jit(solution)/shard_map/ppermute | solution.py:12
  898.0 303.6 %copy-start.222 = (f32[256]{0:T(256)}, f32[256]{0:T(256)S(1)}, u32[]{:S(2)}) copy-start(f32[256]{0:T(256)S(1)} %broadcast_multiply_fusion.2) | copy-start | bytes 3076
  900.9 172.2 %copy-start.190 = (f32[1024]{0:T(1024)S(1)}, f32[1024]{0:T(1024)}, u32[]{:S(2)}) copy-start(f32[1024]{0:T(1024)} %custom-call.18) | copy-start | bytes 12292
  900.9 172.2 %copy-start.191 = (f32[1024]{0:T(1024)S(1)}, f32[1024]{0:T(1024)}, u32[]{:S(2)}) copy-start(f32[1024]{0:T(1024)} %custom-call.19) | copy-start | bytes 12292
  1445.2 5.8 collective-permute-start.3
  1473.8 153.1 %copy-start.111 = (bf16[256,1024]{1,0:T(8,128)(2,1)S(1)}, bf16[256,1024]{1,0:T(8,128)(2,1)}, u32[]{:S(2)}) copy-start(bf16[256,1024]{1,0:T(8,128)(2,1)} %copy-done.109) | copy-start | bytes 1572868
  1473.9 153.1 %copy-start.118 = (bf16[256,1024]{1,0:T(8,128)(2,1)S(1)}, bf16[256,1024]{1,0:T(8,128)(2,1)}, u32[]{:S(2)}) copy-start(bf16[256,1024]{1,0:T(8,128)(2,1)} %copy-done.116) | copy-start | bytes 1572868
  1632.3 205.2 %reduce-scatter.10.cloned.1.call-start = ((), (), s32[]{:S(2)}) async-start(), calls=%async_computation.8 | async-start | bytes 4456448 | tf_op jit(solution)/shard_map/reduce_scatter | solution.py:544
  1639.4 290.8 %reduce-scatter.12.cloned.1.call-start = ((), (), s32[]{:S(2)}) async-start(), calls=%async_computation.9 | async-start | bytes 4456448 | tf_op jit(solution)/shard_map/reduce_scatter | solution.py:545
  1645.9 381.8 %reduce-scatter.14.cloned.1.call-start = ((), (), s32[]{:S(2)}) async-start(), calls=%async_computation.10 | async-start | bytes 4456448 | tf_op jit(solution)/shard_map/reduce_scatter | solution.py:546
  1652.4 472.8 %reduce-scatter.18.cloned.1.call-start = ((), (), s32[]{:S(2)}) async-start(), calls=%async_computation.12 | async-start | bytes 4456448 | tf_op jit(solution)/shard_map/reduce_scatter | solution.py:552
  1658.9 815.0 %reduce-scatter.16.cloned.1.call-start = ((), (), s32[]{:S(2)}) async-start(), calls=%async_computation.11 | async-start | bytes 17825792 | tf_op jit(solution)/shard_map/reduce_scatter | solution.py:551
  1689.9 1138.9 %reduce-scatter.20.cloned.1.call-start = ((), (), s32[]{:S(2)}) async-start(), calls=%async_computation.13 | async-start | bytes 17825792 | tf_op jit(solution)/shard_map/reduce_scatter | solution.py:553
  1747.0 1081.8 %copy-start.1 = (bf16[1,1024,1024]{2,1,0:T(8,128)(2,1)S(1)}, bf16[1,1024,1024]{2,1,0:T(8,128)(2,1)}, u32[]{:S(2)}) copy-start(bf16[1,1024,1024]{2,1,0:T(8,128)(2,1)} %param.50) | copy-start | bytes 6291460
  (342 other events, 1235.4 us)
Sparse Core Ops, SparseCore 0:
  1632.4 99.8 reduce-scatter.7
  1735.2 97.2 reduce-scatter.9
  1835.3 94.8 reduce-scatter.11
  1932.9 94.7 reduce-scatter.13
  2030.4 94.7 reduce-scatter.17
  2127.9 345.9 reduce-scatter.15
  2476.8 351.9 reduce-scatter.19
where the time goes:
time: 2880 us; the launch traced here: 2840 us
  waiting for transfers between devices  993 us (34%)
  other arithmetic  829 us (29%)
  local copies, waits for them, and re-layouts  479 us (17%)
  matrix products  230 us (8%)
  loops' own time  199 us (7%)
  blocking collectives  79.3 us (3%)
    reduce_scatter x1, waiting for transfers between devices, local(): lax.psum_scatter(totals[17], 'dp', scatter_dimension=0, tiled=True)  355 us
    reduce_scatter x1, waiting for transfers between devices, local(): lax.psum_scatter(totals[15], 'dp', scatter_dimension=0, tiled=True)  349 us
    dynamic_update_slice x144, other arithmetic, scaled_lookups(): _, outputs = lax.scan(jax.checkpoint(mix_block), start, pieces)  210 us
    another operation x9, loops' own time, scaled_lookups(): _, outputs = lax.scan(jax.checkpoint(mix_block), start, pieces)  199 us
    dynamic_update_slice x144, local copies, waits for them, and re-layouts, scaled_lookups(): _, outputs = lax.scan(jax.checkpoint(mix_block), start, pieces)  134 us
    eq x144, other arithmetic, mix_block(): doc_block == tail_doc  124 us
    reduce_sum x144, other arithmetic, mix_block(): jnp.sum(linear_attention_routine * content_block_piece[None, :, :], axis=1)  117 us
    squeeze x144, local copies, waits for them, and re-layouts, scaled_lookups(): _, outputs = lax.scan(jax.checkpoint(mix_block), start, pieces)  116 us
  transfers between devices with their start and end apart: 11, of which 6 were waited for; matrix products, arithmetic and copies ran while one was open for 19% of the time, Pallas kernels for 0%

commit v1 on v0

v1 whole, which is shorter than its diff:
```python
import functools

import jax
import jax.numpy as jnp
from jax import lax
from jax.experimental import pallas as pl
from jax.experimental.pallas import tpu as pltpu
from jax.sharding import PartitionSpec as P

BF = jnp.bfloat16
F32 = jnp.float32
LANES = 128


def to_steps(scratch, row, values):
    tokens, width = values.shape
    parts = width // LANES
    for c in range(parts):
        scratch[row, pl.ds(c, tokens, stride=parts), :] = values[:, c * LANES:(c + 1) * LANES]


def column(scratch, row, c, tokens, parts):
    return scratch[row, pl.ds(c, tokens, stride=parts), :]


def recur_forward_kernel(same, fade, bonus, key, value, accept, out, ks, vs):
    rows, tokens, width = key.shape
    parts = width // LANES
    for row in range(rows):
        to_steps(ks, row, key[row])
        to_steps(vs, row, value[row])
    decay = jnp.exp(-jnp.exp(fade[...]))
    extra = bonus[...]

    def step(t, carry):
        at = pl.multiple_of(t * parts, parts)
        following = []
        for row in range(rows):
            top, bottom = carry[2 * row], carry[2 * row + 1]
            m = same[row, t]
            top, bottom = top * m, bottom * m
            k = ks[row, pl.ds(at, parts), :]
            v = vs[row, pl.ds(at, parts), :]
            ek = jnp.exp(k)
            now = jnp.exp(extra + k)
            vs[row, pl.ds(at, parts), :] = (top + now * v) / (bottom + now)
            following += [decay * top + ek * v, decay * bottom + ek]
        return tuple(following)

    zero = jnp.zeros(decay.shape, F32)
    lax.fori_loop(0, tokens, step, (zero,) * (2 * rows), unroll=4)
    for row in range(rows):
        for c in range(parts):
            cols = slice(c * LANES, (c + 1) * LANES)
            y = column(vs, row, c, tokens, parts)
            out[row, :, cols] = (jax.nn.sigmoid(accept[row, :, cols]) * y).astype(BF)


def recur_backward_kernel(same, fade, bonus, key, value, accept, delta, dkey, dvalue, daccept, dfade, dbonus, ks, vs, gs, ys, tops, bottoms):
    rows, tokens, width = key.shape
    parts = width // LANES
    for row in range(rows):
        to_steps(ks, row, key[row])
        to_steps(vs, row, value[row])
        to_steps(gs, row, delta[row] * jax.nn.sigmoid(accept[row]))
    rate = jnp.exp(fade[...])
    decay = jnp.exp(-rate)
    extra = bonus[...]

    def step(t, carry):
        at = pl.multiple_of(t * parts, parts)
        here = pl.ds(at, parts)
        following = []
        for row in range(rows):
            top, bottom = carry[2 * row], carry[2 * row + 1]
            m = same[row, t]
            top, bottom = top * m, bottom * m
            tops[row, here, :] = top
            bottoms[row, here, :] = bottom
            k = ks[row, here, :]
            v = vs[row, here, :]
            ek = jnp.exp(k)
            now = jnp.exp(extra + k)
            inverse = 1.0 / (bottom + now)
            ys[row, here, :] = (top + now * v) * inverse
            gs[row, here, :] = gs[row, here, :] * inverse
            following += [decay * top + ek * v, decay * bottom + ek]
        return tuple(following)

    zero = jnp.zeros(decay.shape, F32)
    lax.fori_loop(0, tokens, step, (zero,) * (2 * rows), unroll=4)

    def back(i, carry):
        t = tokens - 1 - i
        at = pl.multiple_of(t * parts, parts)
        here = pl.ds(at, parts)
        dw, du = carry[:2]
        following = []
        for row in range(rows):
            a, b = carry[2 + 2 * row], carry[3 + 2 * row]
            k = ks[row, here, :]
            v = vs[row, here, :]
            ek = jnp.exp(k)
            now = jnp.exp(extra + k)
            ga = gs[row, here, :]
            gb = -ga * ys[row, here, :]
            q = now * (v * ga + gb)
            ks[row, here, :] = ek * (v * a + b) + q
            vs[row, here, :] = ek * a + now * ga
            du = du + q
            dw = dw + (a * tops[row, here, :] + b * bottoms[row, here, :])
            m = same[row, t]
            following += [(ga + decay * a) * m, (gb + decay * b) * m]
        return (dw, du, *following)

    done = lax.fori_loop(0, tokens, back, (zero,) * (2 + 2 * rows), unroll=4)
    dfade[...] = -done[0] * decay * rate
    dbonus[...] = done[1]
    for row in range(rows):
        for c in range(parts):
            cols = slice(c * LANES, (c + 1) * LANES)
            dkey[row, :, cols] = column(ks, row, c, tokens, parts).astype(BF)
            dvalue[row, :, cols] = column(vs, row, c, tokens, parts).astype(BF)
            gate = jax.nn.sigmoid(accept[row, :, cols])
            y = column(ys, row, c, tokens, parts)
            daccept[row, :, cols] = (delta[row, :, cols] * y * gate * (1.0 - gate)).astype(BF)


def slabs(vector):
    return vector.reshape(vector.shape[0] // LANES, LANES)


def recur_forward(same, fade, bonus, key, value, accept):
    rows, tokens, width = key.shape
    vm = pl.BlockSpec(memory_space=pltpu.VMEM)
    scratch = pltpu.VMEM((rows, tokens * width // LANES, LANES), F32)
    return pl.pallas_call(
        recur_forward_kernel,
        out_shape=jax.ShapeDtypeStruct(key.shape, BF),
        in_specs=[pl.BlockSpec(memory_space=pltpu.SMEM)] + [vm] * 5,
        out_specs=vm,
        scratch_shapes=[scratch] * 2,
        compiler_params=pltpu.CompilerParams(vmem_limit_bytes=40 << 20),
        name="recur_forward",
    )(same, slabs(fade), slabs(bonus), key, value, accept)


def recur_backward(same, fade, bonus, key, value, accept, delta):
    rows, tokens, width = key.shape
    vm = pl.BlockSpec(memory_space=pltpu.VMEM)
    scratch = pltpu.VMEM((rows, tokens * width // LANES, LANES), F32)
    wide = jax.ShapeDtypeStruct(key.shape, BF)
    thin = jax.ShapeDtypeStruct((width // LANES, LANES), F32)
    dkey, dvalue, daccept, dfade, dbonus = pl.pallas_call(
        recur_backward_kernel,
        out_shape=(wide, wide, wide, thin, thin),
        in_specs=[pl.BlockSpec(memory_space=pltpu.SMEM)] + [vm] * 6,
        out_specs=(vm,) * 5,
        scratch_shapes=[scratch] * 6,
        compiler_params=pltpu.CompilerParams(vmem_limit_bytes=48 << 20),
        name="recur_backward",
    )(same, slabs(fade), slabs(bonus), key, value, accept, delta)
    return dkey, dvalue, daccept, dfade.reshape(width), dbonus.reshape(width)


def norm_rows(values, gain, bias):
    centered = values - jnp.mean(values, axis=-1, keepdims=True)
    variance = jnp.mean(centered * centered, axis=-1, keepdims=True)
    return centered * lax.rsqrt(variance + 1e-05) * gain + bias


def previous(values, same):
    before = jnp.concatenate([jnp.zeros_like(values[:, :1]), values[:, :-1]], axis=1)
    return before * same[:, :, None]


def blend(normed, shifted, factor):
    return normed * factor + shifted * (1.0 - factor)


def mixes(values, gain, bias, factors, same):
    normed = norm_rows(values, gain, bias)
    shifted = previous(normed, same)
    return tuple(blend(normed, shifted, f) for f in factors)


def product(left, right):
    return lax.dot_general(left, right, (((2,), (0,)), ((), ())), preferred_element_type=F32)


def back_product(deltas, right):
    return lax.dot_general(deltas, right, (((2,), (1,)), ((), ())), preferred_element_type=F32)


def outer_product(left, right):
    return lax.dot_general(left, right, (((0, 1), (0, 1)), ((), ())), preferred_element_type=F32).astype(BF)


def forward_layer(block_in, same, p):
    (g1, b1, fade, bonus, mk, mv, mr, wk, wv, wr, wo, g2, b2, ck, cr, fk, fr, fv) = p
    state = block_in.astype(F32)
    key_in, value_in, recept_in = (z.astype(BF) for z in mixes(state, g1, b1, (mk, mv, mr), same))
    key = product(key_in, wk)
    value = product(value_in, wv)
    accept = product(recept_in, wr)
    mixed = recur_forward(same, fade, bonus, key, value, accept)
    middle = state + product(mixed, wo)
    hidden_in, gate_in = (z.astype(BF) for z in mixes(middle, g2, b2, (ck, cr), same))
    hidden_pre = product(hidden_in, fk)
    hidden_act = jnp.square(jnp.maximum(hidden_pre, 0.0)).astype(BF)
    hidden_out = product(hidden_act, fv)
    gate_pre = product(gate_in, fr)
    result = (middle + jax.nn.sigmoid(gate_pre) * hidden_out).astype(BF)
    kept = (block_in, key_in, value_in, recept_in, key, value, accept, mixed, middle, hidden_in, gate_in, hidden_pre, hidden_out, gate_pre)
    return result, kept


def backward_layer(incoming, same, p, kept):
    (g1, b1, fade, bonus, mk, mv, mr, wk, wv, wr, wo, g2, b2, ck, cr, fk, fr, fv) = p
    (block_in, key_in, value_in, recept_in, key, value, accept, mixed, middle, hidden_in, gate_in, hidden_pre, hidden_out, gate_pre) = kept
    g = incoming.astype(F32)
    gate = jax.nn.sigmoid(gate_pre)
    delta_out = (g * gate).astype(BF)
    delta_gate = (g * hidden_out * gate * (1.0 - gate)).astype(BF)
    rectified = jnp.maximum(hidden_pre, 0.0)
    hidden_act = jnp.square(rectified).astype(BF)
    delta_pre = (back_product(delta_out, fv) * 2.0 * rectified).astype(BF)
    _, pull = jax.vjp(lambda z, a, b, c, d: mixes(z, a, b, (c, d), same), middle, g2, b2, ck, cr)
    middle_back, dg2, db2, dck, dcr = pull((back_product(delta_pre, fk), back_product(delta_gate, fr)))
    middle_delta = g + middle_back
    delta_branch = middle_delta.astype(BF)
    delta_mixed = back_product(delta_branch, wo)
    delta_key, delta_value, delta_accept, dfade, dbonus = recur_backward(same, fade, bonus, key, value, accept, delta_mixed)
    _, pull = jax.vjp(lambda z, a, b, c, d, e: mixes(z, a, b, (c, d, e), same), block_in.astype(F32), g1, b1, mk, mv, mr)
    state_back, dg1, db1, dmk, dmv, dmr = pull(
        (back_product(delta_key, wk), back_product(delta_value, wv), back_product(delta_accept, wr))
    )
    state_delta = middle_delta + state_back
    vectors = jnp.stack([dg1, db1, dfade, dbonus, dmk, dmv, dmr, dg2, db2, dck, dcr])

    def halves(left, right):
        cut = right.shape[-1] // 2
        return outer_product(left, right[..., :cut]), outer_product(left, right[..., cut:])

    grads = (
        halves(key_in, delta_key),
        halves(value_in, delta_value),
        halves(recept_in, delta_accept),
        halves(mixed, delta_branch),
        halves(hidden_in, delta_pre),
        halves(gate_in, delta_gate),
        halves(hidden_act, delta_out),
    )
    return state_delta, vectors, grads


def halving(blocks, order):
    count = lax.axis_size("dp")
    me = lax.axis_index("dp")
    bits = count.bit_length() - 1
    dims = list(range(bits - 1, -1, -1))
    current = blocks.reshape((2,) * bits + blocks.shape[1:])
    for at, bit in enumerate(order):
        axis = dims.index(bit)
        dims.pop(axis)
        mine = (me >> bit) & 1
        send = lax.dynamic_index_in_dim(current, 1 - mine, axis, keepdims=False)
        keep = lax.dynamic_index_in_dim(current, mine, axis, keepdims=False)
        got = lax.ppermute(send, "dp", [(i, i ^ (1 << bit)) for i in range(count)])
        current = keep.astype(F32) + got.astype(F32)
        if at + 1 < bits:
            current = current.astype(blocks.dtype)
    return current


def local(entry_pair, labels, *params):
    count = lax.axis_size("dp")
    section = lax.axis_index("section")
    own = entry_pair[0]
    p = tuple(e[0].astype(F32) if e.ndim == 2 else e[0] for e in params)
    first = jnp.zeros((labels.shape[0], 1), F32)
    same = jnp.concatenate([first, (labels[:, 1:] == labels[:, :-1]).astype(F32)], axis=1)

    shapes = jax.eval_shape(lambda x: forward_layer(x, same, p), own)
    empty = lambda: jax.tree.map(lambda s: jnp.zeros(s.shape, s.dtype), shapes)
    result, kept = lax.cond(section == 0, lambda: forward_layer(own, same, p), empty)
    received = lax.ppermute(result, "section", [(0, 1)])
    result, kept = lax.cond(section == 1, lambda: forward_layer(received, same, p), lambda: (result, kept))

    back_shapes = jax.eval_shape(lambda g: backward_layer(g, same, p, kept), own)
    empty_back = lambda: jax.tree.map(lambda s: jnp.zeros(s.shape, s.dtype), back_shapes)
    back = lax.cond(section == 1, lambda: backward_layer(own, same, p, kept), empty_back)
    received = lax.ppermute(back[0].astype(BF), "section", [(1, 0)])
    state_delta, vectors, grads = lax.cond(section == 0, lambda: backward_layer(received, same, p, kept), lambda: back)
    block_ends = jnp.where(section == 0, state_delta, result.astype(F32))

    bits = count.bit_length() - 1
    plain = tuple(range(bits))
    turned = (1, 0) + tuple(range(2, bits)) if bits > 1 else plain
    width = vectors.shape[1]
    blocks = vectors.reshape(vectors.shape[0], count, width // count).transpose(1, 0, 2)
    sums = halving(blocks, plain)
    outs = []
    for low, high in grads:
        halves = []
        for piece, order in ((low, plain), (high, turned)):
            halves.append(halving(piece.reshape(count, piece.shape[0] // count, piece.shape[1]), order))
        outs.append(jnp.concatenate(halves, axis=-1))
    gk, gv, gr, go, gfk, gfr, gfv = outs
    v = [sums[i] for i in range(sums.shape[0])]
    everything = (block_ends, *v[:7], gk, gv, gr, go, *v[7:], gfk, gfr, gfv)
    return tuple(e[None] for e in everything)


def solution(mesh):
    vec, mat = P("section", None), P("section", None, None)
    in_specs = (P("section", "dp", None, None), P("dp", None)) + (vec,) * 7 + (mat,) * 4 + (vec,) * 4 + (mat,) * 3
    vec, mat = P("section", "dp"), P("section", "dp", None)
    out_specs = (P("section", "dp", None, None),) + (vec,) * 7 + (mat,) * 4 + (vec,) * 4 + (mat,) * 3
    return jax.shard_map(local, mesh=mesh, in_specs=in_specs, out_specs=out_specs, check_vma=False)
```

time: 2880 us -> 755 us (0.26); the launches traced: 2840 us -> 749 us
  other arithmetic: 829 us -> 77 us
  waiting for transfers between devices: 993 us -> 360 us
  local copies, waits for them, and re-layouts: 479 us -> 125 us
  loops' own time: 199 us -> 8.02 us
  matrix products: 230 us -> 92.7 us
  blocking collectives: 79.3 us -> 0 us
  starting transfers between devices: 9.14 us -> 64.1 us
    reduce_scatter x7 -> x0, waiting for transfers between devices: 991 us -> none  [the longest x1 355 us: local(): lax.psum_scatter(totals[17], 'dp', scatter_dimension=0, tiled=True)]
    ppermute x4 -> x62, waiting for transfers between devices: 1.5 us -> 360 us  [the longest x60 196 us: halving(): got = lax.ppermute(send, 'dp', [(i, i ^ 1 << bit) for i in range(count)])]
    reduce_sum x405 -> x6, other arithmetic: 309 us -> 11.3 us  [the longest x2 4.57 us: norm_rows(): return centered * lax.rsqrt(variance + 1e-05) * gain + bias]
    dynamic_update_slice x144 -> x0, other arithmetic: 210 us -> none  [scaled_lookups(): _, outputs = lax.scan(jax.checkpoint(mix_block), start, pieces)]
    another operation x9 -> x4, loops' own time: 199 us -> 8.02 us  [the longest x1 3.39 us: local(): lax.cond(section == 1, lambda: forward_layer(received, same, p), lambda:...]
    eq x241 -> x1, other arithmetic: 171 us -> 0.83 us  [local(): labels[:, 1:] == labels[:, :-1]]
    dot_general x63 -> x28, matrix products: 230 us -> 92.7 us  [the longest x14 38.1 us: outer_product(): lax.dot_general(left, right, (((0, 1), (0, 1)), ((), ())), preferred_elem...]
    dynamic_update_slice x144 -> x0, local copies, waits for them, and re-layouts: 134 us -> none  [scaled_lookups(): _, outputs = lax.scan(jax.checkpoint(mix_block), start, pieces)]
  transfers between devices with their start and end apart: 11 -> 62, of which waited for: 6 -> 47; matrix products, arithmetic and copies ran while one was open for 19% -> 8% of each run, Pallas kernels for 0% -> 0%
where the time goes in v1:
time: 755 us; the launch traced here: 749 us
  waiting for transfers between devices  360 us (48%)
  local copies, waits for them, and re-layouts  125 us (17%)
  matrix products  92.7 us (12%)
  other arithmetic  77 us (10%)
  starting transfers between devices  64.1 us (8%)
  Pallas kernels  19.3 us (3%)
  loops' own time  8.02 us (1%)
    ppermute x60, waiting for transfers between devices, halving(): got = lax.ppermute(send, 'dp', [(i, i ^ 1 << bit) for i in range(count)])  196 us
    ppermute x1, waiting for transfers between devices, local(): received = lax.ppermute(back[0].astype(BF), 'section', [(1, 0)])  162 us
    ppermute x60, starting transfers between devices, halving(): got = lax.ppermute(send, 'dp', [(i, i ^ 1 << bit) for i in range(count)])  61.5 us
    cond x109, local copies, waits for them, and re-layouts  50.7 us
    dot_general x14, matrix products, outer_product(): lax.dot_general(left, right, (((0, 1), (0, 1)), ((), ())), preferred_elem...  38.1 us
    squeeze x56, local copies, waits for them, and re-layouts, halving(): send = lax.dynamic_index_in_dim(current, 1 - mine, axis, keepdims=False)  29.4 us
    dot_general x7, matrix products, product(): lax.dot_general(left, right, (((2,), (0,)), ((), ())), preferred_element_...  29.4 us
    dot_general x7, matrix products, back_product(): lax.dot_general(deltas, right, (((2,), (1,)), ((), ())), preferred_elemen...  25.1 us
  transfers between devices with their start and end apart: 62, of which 47 were waited for; matrix products, arithmetic and copies ran while one was open for 8% of the time, Pallas kernels for 0%

profile of v1, /device:TPU:0, one launch (start us, length us, event | category | flops | bytes accessed | tf_op | source)
XLA Modules:
  0.0 748.9 jit_solution(5364820464034955770)
XLA Ops:
  9.2 48.1 %conditional.4 = (bf16[2,256,1024]{2,1,0:T(8,128)(2,1)}, bf16[2,256,1024]{2,1,0:T(8,128)(2,1)S(1)}, bf16[2,256,1024]{2,1,0:T(8,128)(2,1)S(1)}, bf16[2,256,1024]{...) conditional(s32[]{:T(128)} %convert_element_type.960, ...), branch_computations={%region_0.0_spmd, %region_1.0_spmd} | conditional | flops 13995350016 | bytes 213009024 | solution.py:286
  23.1 6.9 recur_forward.2
  35.4 7.0 fusion.2
  43.7 12.1 %add_convert_fusion = (bf16[2,256,1024]{2,1,0:T(8,128)(2,1)}, f32[2,256,1024]{2,1,0:T(8,128)S(1)}) fusion(f32[2,256,1024]{2,1,0:T(8,128)S(1)} %get-tuple-element.1072, f32[2,256,1024]{2,1,0:T(8,128)S(1)} %fusion.10, bf16[4096,1024]{1,0:T(8,128)(2,1)} %get-tuple-element.420, f32[2,256,4096]{2,1,0:T(8,128)} %fusion.2), kind=kOutput, calls=%fused_computation.24 | convolution fusion | flops 4304404480 | bytes 24117248 | tf_op jit(solution)/shard_map/cond/branch_1_fun/dot_general | solution.py:188
  67.9 25.1 %conditional.6 = (f32[2,256,1024]{2,1,0:T(8,128)}, f32[11,1024]{1,0:T(8,128)S(1)}, bf16[4096,512]{1,0:T(8,128)(2,1)}, bf16[4096,512]{1,0:T(8,128)(2,1)}, bf16[10...) conditional(s32[]{:T(128)} %convert_element_type.961, ...), branch_computations={%region_12.0_spmd, %region_13.36_spmd} | conditional | flops 28014264320 | bytes 441787360 | solution.py:292
  97.2 162.0 %collective-permute-done.1 = bf16[2,256,1024]{2,1,0:T(8,128)(2,1)} collective-permute-done((bf16[2,256,1024]{2,1,0:T(8,128)(2,1)}, bf16[2,256,1024]{2,1,0:T(8,128)(2,1)}, u32[]{:S(2)}, u32[]{:S(2)}) %collective-permute-start.1) | collective-permute-done | bytes 1048608 | tf_op jit(solution)/shard_map/ppermute | solution.py:293
  259.2 167.2 %conditional.7 = (f32[2,256,1024]{2,1,0:T(8,128)}, f32[11,1024]{1,0:T(8,128)S(1)}, bf16[2,2,2,2,64,512]{5,4,3,2,1,0:T(8,128)(2,1)}, bf16[2,2,2,2,64,512]{5,4,3,2...) conditional(s32[]{:T(128)} %convert_element_type.960, ...), branch_computations={%region_36.37_spmd, %region_37.60_spmd} | conditional | flops 28014264320 | bytes 496313472 | solution.py:294
  263.3 10.2 %multiply_convert_fusion.9 = bf16[2,256,4096]{2,1,0:T(8,128)(2,1)S(1)} fusion(f32[2,256,4096]{2,1,0:T(8,128)} %get-tuple-element.486, bf16[2,256,1024]{2,1,0:T(8,128)(2,1)S(1)} %get-tuple-element.1020, bf16[4096,1024]{1,0:T(8,128)(2,1)} %get-tuple-element.485), kind=kOutput, calls=%fused_computation.228 | convolution fusion | flops 4303355904 | bytes 22020096 | tf_op jit(solution)/shard_map/cond/branch_1_fun/dot_general | solution.py:192
  273.6 8.5 %fusion.113 = f32[2,256,1024]{2,1,0:T(8,128)S(1)} fusion(bf16[2,256,4096]{2,1,0:T(8,128)(2,1)S(1)} %multiply_convert_fusion.9, bf16[1024,4096]{1,0:T(8,128)(2,1)} %get-tuple-element.487), kind=kOutput, calls=%fused_computation.223 | convolution fusion | flops 4294967296 | bytes 14680064 | tf_op jit(solution)/shard_map/cond/branch_1_fun/dot_general | solution.py:192
  295.4 12.5 %recur_backward.3 = (bf16[2,256,1024]{2,1,0:T(8,128)(2,1)S(1)}, bf16[2,256,1024]{2,1,0:T(8,128)(2,1)S(1)}, bf16[2,256,1024]{2,1,0:T(8,128)(2,1)S(1)}, f32[8,128]{1,0:T(8,128)S(1)}, f32[8,128]{1,0:T(8,128)S(1)}) custom-call(f32[2,256]{1,0:T(2,128)S(1)} %get-tuple-element.489.same, f32[8,128]{1,0:T(8,128)S(1)} %bitcast.760, f32[8,128]{1,0:T(8,128)S(1)} %bitcast.768, ...), custom_call_target="tpu_custom_call" | custom-call | tf_op jit(solution)/shard_map/cond/branch_1_fun/recur_backward/pallas_call | solution.py:154
  321.6 5.2 add_add_fusion.5
  370.3 6.0 bitcast_convert_fusion.17
  385.7 4.9 copy.407
  390.6 7.7 %bitcast_convert_fusion.15 = bf16[4096,512]{1,0:T(8,128)(2,1)} fusion(f32[2,256,4096]{2,1,0:T(8,128)} %get-tuple-element.486, bf16[2,256,1024]{2,1,0:T(8,128)(2,1)S(1)} %copy-done.37), kind=kOutput, calls=%fused_computation.220 | convolution fusion | flops 2155872256 | bytes 13107200 | tf_op jit(solution)/shard_map/cond/branch_1_fun/dot_general | solution.py:196
  402.9 7.8 %bitcast_convert_fusion.14 = bf16[4096,512]{1,0:T(8,128)(2,1)} fusion(f32[2,256,4096]{2,1,0:T(8,128)} %get-tuple-element.486, bf16[2,256,1024]{2,1,0:T(8,128)(2,1)S(1)} %copy-done.37), kind=kOutput, calls=%fused_computation.219 | convolution fusion | flops 2155872256 | bytes 13107200 | tf_op jit(solution)/shard_map/cond/branch_1_fun/dot_general | solution.py:196
  466.0 7.5 %collective-permute-done.3 = f32[2,2,11,64]{3,1,2,0:T(2,128)S(1)} collective-permute-done((f32[2,2,11,64]{3,1,2,0:T(2,128)S(1)}, f32[2,2,11,64]{3,1,2,0:T(2,128)S(1)}, u32[]{:S(2)}, u32[]{:S(2)}) %collective-permute-start.3) | collective-permute-done | bytes 11296 | tf_op jit(solution)/shard_map/ppermute | solution.py:269
  520.4 33.6 %collective-permute-done.51 = bf16[2,2,64,512]{3,2,0,1:T(8,128)(2,1)S(1)} collective-permute-done((bf16[2,2,64,512]{3,2,0,1:T(8,128)(2,1)S(1)}, bf16[2,2,64,512]{3,2,0,1:T(8,128)(2,1)S(1)}, u32[]{:S(2)}, u32[]{:S(2)}) %collective-permute-start.51) | collective-permute-done | bytes 262176 | tf_op jit(solution)/shard_map/ppermute | solution.py:269
  581.4 7.3 collective-permute-done.48
  598.7 4.9 collective-permute-done.36
  603.6 4.9 collective-permute-done.24
  707.9 7.3 collective-permute-done.39
  722.7 7.8 %collective-permute-done.40 = bf16[2,64,2048]{2,1,0:T(8,128)(2,1)S(1)} collective-permute-done((bf16[2,64,2048]{2,1,0:T(8,128)(2,1)S(1)}, bf16[2,64,2048]{2,1,0:T(8,128)(2,1)S(1)}, u32[]{:S(2)}, u32[]{:S(2)}) %collective-permute-start.40) | collective-permute-done | bytes 524320 | tf_op jit(solution)/shard_map/ppermute | solution.py:269
  731.0 5.2 collective-permute-done.44
  736.8 8.0 %collective-permute-done.41 = bf16[64,2048]{1,0:T(8,128)(2,1)S(1)} collective-permute-done((bf16[64,2048]{1,0:T(8,128)(2,1)S(1)}, bf16[64,2048]{1,0:T(8,128)(2,1)S(1)}, u32[]{:S(2)}, u32[]{:S(2)}) %collective-permute-start.41) | collective-permute-done | bytes 262176 | tf_op jit(solution)/shard_map/ppermute | solution.py:269
  (485 shorter events, 405.2 us)
Async XLA Ops:
  95.9 163.3 %collective-permute-start.1 = (bf16[2,256,1024]{2,1,0:T(8,128)(2,1)}, bf16[2,256,1024]{2,1,0:T(8,128)(2,1)}, u32[]{:S(2)}, u32[]{:S(2)}) collective-permute-start(bf16[2,256,1024]{2,1,0:T(8,128)(2,1)} %convert_element_type.984), channel_id=1, source_target_pairs={{16,0},{17,1},{18,2},{19,3},{20,4},{21,5},{22,6},{23,7},{24,8},{25... | collective-permute-start | bytes 3145736 | tf_op jit(solution)/shard_map/ppermute | solution.py:293
  429.5 256.6 %collective-permute-start.54 = (bf16[2,2,2,256,512]{4,3,0,1,2:T(8,128)(2,1)}, bf16[2,2,2,256,512]{4,3,0,1,2:T(8,128)(2,1)}, u32[]{:S(2)}, u32[]{:S(2)}) collective-permute-start(bf16[2,2,2,256,512]{4,3,0,1,2:T(8,128)(2,1)} %copy_bitcast_fusion.1), channel_id=1, source_target_pairs={{0,1},{1,0},{2,3},{3,2},{4,5},{5,4},{6,7},{7,6},{8,9},{9,8},{10,11... | collective-permute-start | bytes 6291464 | tf_op jit(solution)/shard_map/ppermute | solution.py:269
  435.4 254.2 %collective-permute-start.58 = (bf16[2,2,2,256,512]{4,3,0,1,2:T(8,128)(2,1)}, bf16[2,2,2,256,512]{4,3,0,1,2:T(8,128)(2,1)}, u32[]{:S(2)}, u32[]{:S(2)}) collective-permute-start(bf16[2,2,2,256,512]{4,3,0,1,2:T(8,128)(2,1)} %copy_bitcast_fusion), channel_id=1, source_target_pairs={{0,2},{1,3},{2,0},{3,1},{4,6},{5,7},{6,4},{7,5},{8,10},{9,11},{10,... | collective-permute-start | bytes 6291464 | tf_op jit(solution)/shard_map/ppermute | solution.py:269
  438.8 45.6 %collective-permute-start.46 = (bf16[2,2,2,64,512]{4,3,0,1,2:T(8,128)(2,1)}, bf16[2,2,2,64,512]{4,3,0,1,2:T(8,128)(2,1)S(1)}, u32[]{:S(2)}, u32[]{:S(2)}) collective-permute-start(bf16[2,2,2,64,512]{4,3,0,1,2:T(8,128)(2,1)} %copy_bitcast_fusion.5), channel_id=1, source_target_pairs={{0,1},{1,0},{2,3},{3,2},{4,5},{5,4},{6,7},{7,6},{8,9},{9,8},{10,11... | collective-permute-start | bytes 1572872 | tf_op jit(solution)/shard_map/ppermute | solution.py:269
  441.2 45.9 %collective-permute-start.50 = (bf16[2,2,2,64,512]{4,3,0,1,2:T(8,128)(2,1)}, bf16[2,2,2,64,512]{4,3,0,1,2:T(8,128)(2,1)S(1)}, u32[]{:S(2)}, u32[]{:S(2)}) collective-permute-start(bf16[2,2,2,64,512]{4,3,0,1,2:T(8,128)(2,1)} %copy_bitcast_fusion.4), channel_id=1, source_target_pairs={{0,2},{1,3},{2,0},{3,1},{4,6},{5,7},{6,4},{7,5},{8,10},{9,11},{10,... | collective-permute-start | bytes 1572872 | tf_op jit(solution)/shard_map/ppermute | solution.py:269
  462.8 10.7 %collective-permute-start.3 = (f32[2,2,11,64]{3,1,2,0:T(2,128)S(1)}, f32[2,2,11,64]{3,1,2,0:T(2,128)S(1)}, u32[]{:S(2)}, u32[]{:S(2)}) collective-permute-start(f32[2,2,11,64]{3,1,2,0:T(2,128)S(1)} %bitcast.770), channel_id=1, source_target_pairs={{0,2},{1,3},{2,0},{3,1},{4,6},{5,7},{6,4},{7,5},{8,10},{9,11},{10,... | collective-permute-start | bytes 33800 | tf_op jit(solution)/shard_map/ppermute | solution.py:269
  484.4 9.6 %collective-permute-start.34 = (bf16[2,2,2,64,512]{4,3,0,1,2:T(8,128)(2,1)S(1)}, bf16[2,2,2,64,512]{4,3,0,1,2:T(8,128)(2,1)S(1)}, u32[]{:S(2)}, u32[]{:S(2)}) collective-permute-start(bf16[2,2,2,64,512]{4,3,0,1,2:T(8,128)(2,1)S(1)} %copy-done.75), channel_id=1, source_target_pairs={{0,2},{1,3},{2,0},{3,1},{4,6},{5,7},{6,4},{7,5},{8,10},{9,11},{10,... | collective-permute-start | bytes 1572872 | tf_op jit(solution)/shard_map/ppermute | solution.py:269
  487.2 9.9 %collective-permute-start.22 = (bf16[2,2,2,64,512]{4,3,0,1,2:T(8,128)(2,1)S(1)}, bf16[2,2,2,64,512]{4,3,0,1,2:T(8,128)(2,1)S(1)}, u32[]{:S(2)}, u32[]{:S(2)}) collective-permute-start(bf16[2,2,2,64,512]{4,3,0,1,2:T(8,128)(2,1)S(1)} %copy-done.74), channel_id=1, source_target_pairs={{0,1},{1,0},{2,3},{3,2},{4,5},{5,4},{6,7},{7,6},{8,9},{9,8},{10,11... | collective-permute-start | bytes 1572872 | tf_op jit(solution)/shard_map/ppermute | solution.py:269
  506.7 186.4 %collective-permute-start.38 = (bf16[2,2,2,64,2048]{4,3,0,1,2:T(8,128)(2,1)S(1)}, bf16[2,2,2,64,2048]{4,3,0,1,2:T(8,128)(2,1)S(1)}, u32[]{:S(2)}, u32[]{:S(2)}) collective-permute-start(bf16[2,2,2,64,2048]{4,3,0,1,2:T(8,128)(2,1)S(1)} %copy-done.33), channel_id=1, source_target_pairs={{0,1},{1,0},{2,3},{3,2},{4,5},{5,4},{6,7},{7,6},{8,9},{9,8},{10,11... | collective-permute-start | bytes 6291464 | tf_op jit(solution)/shard_map/ppermute | solution.py:269
  512.6 41.3 %collective-permute-start.51 = (bf16[2,2,64,512]{3,2,0,1:T(8,128)(2,1)S(1)}, bf16[2,2,64,512]{3,2,0,1:T(8,128)(2,1)S(1)}, u32[]{:S(2)}, u32[]{:S(2)}) collective-permute-start(bf16[2,2,64,512]{3,2,0,1:T(8,128)(2,1)S(1)} %dynamic-slice_bitcast_fusion.10), channel_id=1, source_target_pairs={{0,1},{1,0},{2,3},{3,2},{4,5},{5,4},{6,7},{7,6},{8,9},{9,8},{10,11... | collective-permute-start | bytes 786440 | tf_op jit(solution)/shard_map/ppermute | solution.py:269
  518.8 36.8 %collective-permute-start.31 = (bf16[2,2,64,512]{3,2,0,1:T(8,128)(2,1)S(1)}, bf16[2,2,64,512]{3,2,0,1:T(8,128)(2,1)S(1)}, u32[]{:S(2)}, u32[]{:S(2)}) collective-permute-start(bf16[2,2,64,512]{3,2,0,1:T(8,128)(2,1)S(1)} %dynamic-slice_bitcast_fusion.15), channel_id=1, source_target_pairs={{0,2},{1,3},{2,0},{3,1},{4,6},{5,7},{6,4},{7,5},{8,10},{9,11},{10,... | collective-permute-start | bytes 786440 | tf_op jit(solution)/shard_map/ppermute | solution.py:269
  575.5 121.9 %collective-permute-start.42 = (bf16[2,2,2,64,2048]{4,3,0,1,2:T(8,128)(2,1)S(1)}, bf16[2,2,2,64,2048]{4,3,0,1,2:T(8,128)(2,1)S(1)}, u32[]{:S(2)}, u32[]{:S(2)}) collective-permute-start(bf16[2,2,2,64,2048]{4,3,0,1,2:T(8,128)(2,1)S(1)} %copy-done.32), channel_id=1, source_target_pairs={{0,2},{1,3},{2,0},{3,1},{4,6},{5,7},{6,4},{7,5},{8,10},{9,11},{10,... | collective-permute-start | bytes 6291464 | tf_op jit(solution)/shard_map/ppermute | solution.py:269
  689.1 14.9 %collective-permute-start.55 = (bf16[2,2,256,512]{3,2,0,1:T(8,128)(2,1)S(1)}, bf16[2,2,256,512]{3,2,0,1:T(8,128)(2,1)S(1)}, u32[]{:S(2)}, u32[]{:S(2)}) collective-permute-start(bf16[2,2,256,512]{3,2,0,1:T(8,128)(2,1)S(1)} %dynamic-slice_bitcast_fusion.1), channel_id=1, source_target_pairs={{0,2},{1,3},{2,0},{3,1},{4,6},{5,7},{6,4},{7,5},{8,10},{9,11},{10,... | collective-permute-start | bytes 3145736 | tf_op jit(solution)/shard_map/ppermute | solution.py:269
  692.6 14.9 %collective-permute-start.59 = (bf16[2,2,256,512]{3,2,0,1:T(8,128)(2,1)S(1)}, bf16[2,2,256,512]{3,2,0,1:T(8,128)(2,1)S(1)}, u32[]{:S(2)}, u32[]{:S(2)}) collective-permute-start(bf16[2,2,256,512]{3,2,0,1:T(8,128)(2,1)S(1)} %dynamic-slice_bitcast_fusion), channel_id=1, source_target_pairs={{0,1},{1,0},{2,3},{3,2},{4,5},{5,4},{6,7},{7,6},{8,9},{9,8},{10,11... | collective-permute-start | bytes 3145736 | tf_op jit(solution)/shard_map/ppermute | solution.py:269
  695.6 19.6 %collective-permute-start.39 = (bf16[2,2,64,2048]{3,2,0,1:T(8,128)(2,1)S(1)}, bf16[2,2,64,2048]{3,2,0,1:T(8,128)(2,1)S(1)}, u32[]{:S(2)}, u32[]{:S(2)}) collective-permute-start(bf16[2,2,64,2048]{3,2,0,1:T(8,128)(2,1)S(1)} %dynamic-slice_bitcast_fusion.3), channel_id=1, source_target_pairs={{0,2},{1,3},{2,0},{3,1},{4,6},{5,7},{6,4},{7,5},{8,10},{9,11},{10,... | collective-permute-start | bytes 3145736 | tf_op jit(solution)/shard_map/ppermute | solution.py:269
  700.1 18.6 %collective-permute-start.43 = (bf16[2,2,64,2048]{3,2,0,1:T(8,128)(2,1)S(1)}, bf16[2,2,64,2048]{3,2,0,1:T(8,128)(2,1)S(1)}, u32[]{:S(2)}, u32[]{:S(2)}) collective-permute-start(bf16[2,2,64,2048]{3,2,0,1:T(8,128)(2,1)S(1)} %dynamic-slice_bitcast_fusion.2), channel_id=1, source_target_pairs={{0,1},{1,0},{2,3},{3,2},{4,5},{5,4},{6,7},{7,6},{8,9},{9,8},{10,11... | collective-permute-start | bytes 3145736 | tf_op jit(solution)/shard_map/ppermute | solution.py:269
  704.3 15.0 %collective-permute-start.56 = (bf16[2,256,512]{2,1,0:T(8,128)(2,1)S(1)}, bf16[2,256,512]{2,1,0:T(8,128)(2,1)S(1)}, u32[]{:S(2)}, u32[]{:S(2)}) collective-permute-start(bf16[2,256,512]{2,1,0:T(8,128)(2,1)S(1)} %dynamic-slice_bitcast_fusion.5), channel_id=1, source_target_pairs={{0,4},{1,5},{2,6},{3,7},{4,0},{5,1},{6,2},{7,3},{8,12},{9,13},{10,... | collective-permute-start | bytes 1572872 | tf_op jit(solution)/shard_map/ppermute | solution.py:269
  707.8 14.4 %collective-permute-start.60 = (bf16[2,256,512]{2,1,0:T(8,128)(2,1)S(1)}, bf16[2,256,512]{2,1,0:T(8,128)(2,1)S(1)}, u32[]{:S(2)}, u32[]{:S(2)}) collective-permute-start(bf16[2,256,512]{2,1,0:T(8,128)(2,1)S(1)} %dynamic-slice_bitcast_fusion.4), channel_id=1, source_target_pairs={{0,4},{1,5},{2,6},{3,7},{4,0},{5,1},{6,2},{7,3},{8,12},{9,13},{10,... | collective-permute-start | bytes 1572872 | tf_op jit(solution)/shard_map/ppermute | solution.py:269
  715.6 14.9 %collective-permute-start.40 = (bf16[2,64,2048]{2,1,0:T(8,128)(2,1)S(1)}, bf16[2,64,2048]{2,1,0:T(8,128)(2,1)S(1)}, u32[]{:S(2)}, u32[]{:S(2)}) collective-permute-start(bf16[2,64,2048]{2,1,0:T(8,128)(2,1)S(1)} %dynamic-slice_bitcast_fusion.7), channel_id=1, source_target_pairs={{0,4},{1,5},{2,6},{3,7},{4,0},{5,1},{6,2},{7,3},{8,12},{9,13},{10,... | collective-permute-start | bytes 1572872 | tf_op jit(solution)/shard_map/ppermute | solution.py:269
  719.2 17.0 %collective-permute-start.44 = (bf16[2,64,2048]{2,1,0:T(8,128)(2,1)S(1)}, bf16[2,64,2048]{2,1,0:T(8,128)(2,1)S(1)}, u32[]{:S(2)}, u32[]{:S(2)}) collective-permute-start(bf16[2,64,2048]{2,1,0:T(8,128)(2,1)S(1)} %dynamic-slice_bitcast_fusion.6), channel_id=1, source_target_pairs={{0,4},{1,5},{2,6},{3,7},{4,0},{5,1},{6,2},{7,3},{8,12},{9,13},{10,... | collective-permute-start | bytes 1572872 | tf_op jit(solution)/shard_map/ppermute | solution.py:269
  719.4 25.4 %collective-permute-start.57 = (bf16[256,512]{1,0:T(8,128)(2,1)S(1)}, bf16[256,512]{1,0:T(8,128)(2,1)S(1)}, u32[]{:S(2)}, u32[]{:S(2)}) collective-permute-start(bf16[256,512]{1,0:T(8,128)(2,1)S(1)} %dynamic-slice_bitcast_fusion.9), channel_id=1, source_target_pairs={{0,8},{1,9},{2,10},{3,11},{4,12},{5,13},{6,14},{7,15},{8,0},{9,1},... | collective-permute-start | bytes 786440 | tf_op jit(solution)/shard_map/ppermute | solution.py:269
  722.4 22.5 %collective-permute-start.61 = (bf16[256,512]{1,0:T(8,128)(2,1)S(1)}, bf16[256,512]{1,0:T(8,128)(2,1)S(1)}, u32[]{:S(2)}, u32[]{:S(2)}) collective-permute-start(bf16[256,512]{1,0:T(8,128)(2,1)S(1)} %dynamic-slice_bitcast_fusion.8), channel_id=1, source_target_pairs={{0,8},{1,9},{2,10},{3,11},{4,12},{5,13},{6,14},{7,15},{8,0},{9,1},... | collective-permute-start | bytes 786440 | tf_op jit(solution)/shard_map/ppermute | solution.py:269
  730.7 14.1 %collective-permute-start.41 = (bf16[64,2048]{1,0:T(8,128)(2,1)S(1)}, bf16[64,2048]{1,0:T(8,128)(2,1)S(1)}, u32[]{:S(2)}, u32[]{:S(2)}) collective-permute-start(bf16[64,2048]{1,0:T(8,128)(2,1)S(1)} %dynamic-slice_bitcast_fusion.13), channel_id=1, source_target_pairs={{0,8},{1,9},{2,10},{3,11},{4,12},{5,13},{6,14},{7,15},{8,0},{9,1},... | collective-permute-start | bytes 786440 | tf_op jit(solution)/shard_map/ppermute | solution.py:269
  736.4 11.2 %collective-permute-start.45 = (bf16[64,2048]{1,0:T(8,128)(2,1)S(1)}, bf16[64,2048]{1,0:T(8,128)(2,1)S(1)}, u32[]{:S(2)}, u32[]{:S(2)}) collective-permute-start(bf16[64,2048]{1,0:T(8,128)(2,1)S(1)} %dynamic-slice_bitcast_fusion.12), channel_id=1, source_target_pairs={{0,8},{1,9},{2,10},{3,11},{4,12},{5,13},{6,14},{7,15},{8,0},{9,1},... | collective-permute-start | bytes 786440 | tf_op jit(solution)/shard_map/ppermute | solution.py:269
  (97 other events, 900.9 us)

commit v2 on v1

v2 whole, which is shorter than its diff:
```python
import functools

import jax
import jax.numpy as jnp
from jax import lax
from jax.experimental import pallas as pl
from jax.experimental.pallas import tpu as pltpu
from jax.sharding import PartitionSpec as P

BF = jnp.bfloat16
F32 = jnp.float32
LANES = 128
VM = pl.BlockSpec(memory_space=pltpu.VMEM)
HBM = pl.BlockSpec(memory_space=pl.ANY)
SM = pl.BlockSpec(memory_space=pltpu.SMEM)

def dot(left, right):
    return jnp.dot(left, right, preferred_element_type=F32)

def dot_nt(left, right):
    return lax.dot_general(left, right, (((1,), (1,)), ((), ())), preferred_element_type=F32)

def lanes(c):
    return pl.ds(pl.multiple_of(c * LANES, LANES), LANES)

def statistics(source, mean, scale, tokens, width, chunk=64):
    def step(i, _):
        at = pl.ds(pl.multiple_of(i * chunk, chunk), chunk)
        x = source[at, :].astype(F32)
        m = jnp.sum(x, axis=1, keepdims=True) * (1.0 / width)
        x = x - m
        v = jnp.sum(x * x, axis=1, keepdims=True) * (1.0 / width)
        mean[at, :] = jnp.broadcast_to(m, (chunk, LANES))
        scale[at, :] = jnp.broadcast_to(lax.rsqrt(v + 1e-05), (chunk, LANES))
        return 0
    lax.fori_loop(0, tokens // chunk, step, 0)

def mix_into(source, mean, scale, same, gain, bias, factors, targets, width):
    def step(c, _):
        cols = lanes(c)
        z = (source[:, cols].astype(F32) - mean[...]) * scale[...] * gain[:, cols].astype(F32) + bias[:, cols].astype(F32)
        before = pltpu.roll(z, 1, 0) * same[...]
        step_up = z - before
        for factor, target in zip(factors, targets):
            target[:, cols] = (before + step_up * factor[:, cols].astype(F32)).astype(BF)
        return 0
    lax.fori_loop(0, width // LANES, step, 0)

def fetch(pairs, sems):
    copies = [pltpu.make_async_copy(s, d, sems.at[i]) for i, (s, d) in enumerate(pairs)]
    for c in copies:
        c.start()
    return copies

def forward_kernel(rows, with_delta, *refs):
    (same_s, same, h, g1, b1, fade, bonus, mk, mv, mr, g2, b2, ck, cr, cot) = refs[:15]
    weights = refs[15:22]
    n_out = 15
    outs = refs[22:22 + n_out]
    (wk, wv, wr, wo, fk, fr, fv, mean, scale, key_in, value_in, recept_in, ks, vs, ys, gate, mixed, middle,
     hidden_in, gate_in, rect, act, delta_out, delta_gate, result, in_sems, out_sems) = refs[22 + n_out:]
    tokens, width = h.shape
    each = tokens // rows
    parts = width // LANES
    tile = 512
    ff = rect.shape[1]
    loads = fetch(list(zip(weights, (wk, wv, wr, wo, fk, fr, fv))), in_sems)
    saves = []

    def save(source):
        i = len(saves)
        saves.append(pltpu.make_async_copy(source, outs[i], out_sems.at[i]))
        saves[-1].start()

    statistics(h, mean, scale, tokens, width)
    mix_into(h, mean, scale, same, g1, b1, (mk, mv, mr), (key_in, value_in, recept_in), width)
    for z in (key_in, value_in, recept_in):
        save(z)

    def cols_of(j):
        return pl.ds(pl.multiple_of(j * tile, tile), tile)

    def steps_tile(values, target, j):
        for row in range(rows):
            for c in range(tile // LANES):
                target[pl.ds(row * each * parts + j * (tile // LANES) + c, each, stride=parts), :] = values[row * each:(row + 1) * each, c * LANES:(c + 1) * LANES]

    loads[0].wait()
    def key_tile(j, _):
        steps_tile(dot(key_in[...], wk[:, cols_of(j)]), ks, j)
        return 0
    lax.fori_loop(0, width // tile, key_tile, 0)
    loads[1].wait()
    def value_tile(j, _):
        steps_tile(dot(value_in[...], wv[:, cols_of(j)]), vs, j)
        return 0
    lax.fori_loop(0, width // tile, value_tile, 0)
    save(ks)
    save(vs)
    loads[2].wait()
    def accept_tile(j, _):
        gate[:, cols_of(j)] = jax.nn.sigmoid(dot(recept_in[...], wr[:, cols_of(j)]))
        return 0
    lax.fori_loop(0, width // tile, accept_tile, 0)
    save(gate)

    decay = jnp.exp(-jnp.exp(fade[...]))
    extra = bonus[...]
    def step(t, carry):
        following = []
        for row in range(rows):
            here = pl.ds(pl.multiple_of((row * each + t) * parts, parts), parts)
            m = same_s[row, t]
            top, bottom = carry[2 * row] * m, carry[2 * row + 1] * m
            k, v = ks[here, :], vs[here, :]
            ek, now = jnp.exp(k), jnp.exp(extra + k)
            ys[here, :] = (top + now * v) / (bottom + now)
            following += [decay * top + ek * v, decay * bottom + ek]
        return tuple(following)
    zero = jnp.zeros(decay.shape, F32)
    lax.fori_loop(0, each, step, (zero,) * (2 * rows), unroll=4)

    for row in range(rows):
        def mixed_step(c, _, row=row):
            y = ys[pl.ds(row * each * parts + c, each, stride=parts), :]
            mixed[row * each:(row + 1) * each, lanes(c)] = (gate[row * each:(row + 1) * each, lanes(c)] * y).astype(BF)
            return 0
        lax.fori_loop(0, parts, mixed_step, 0)
    save(mixed)
    loads[3].wait()
    def middle_tile(j, _):
        middle[:, cols_of(j)] = h[:, cols_of(j)].astype(F32) + dot(mixed[...], wo[:, cols_of(j)])
        return 0
    lax.fori_loop(0, width // tile, middle_tile, 0)
    save(middle)

    statistics(middle, mean, scale, tokens, width)
    mix_into(middle, mean, scale, same, g2, b2, (ck, cr), (hidden_in, gate_in), width)
    save(hidden_in)
    save(gate_in)
    loads[4].wait()
    def hidden_tile(j, _):
        r = jnp.maximum(dot(hidden_in[...], fk[:, cols_of(j)]), 0.0)
        rect[:, cols_of(j)] = r.astype(BF)
        act[:, cols_of(j)] = (r * r).astype(BF)
        return 0
    lax.fori_loop(0, ff // tile, hidden_tile, 0)
    save(rect)
    save(act)
    saves[5].wait()
    loads[5].wait()
    def gate_tile(j, _):
        gate[:, cols_of(j)] = jax.nn.sigmoid(dot(gate_in[...], fr[:, cols_of(j)]))
        return 0
    lax.fori_loop(0, width // tile, gate_tile, 0)
    loads[6].wait()
    def out_tile(j, _):
        cols = cols_of(j)
        o = dot(act[...], fv[:, cols])
        s = gate[:, cols]
        result[:, cols] = (middle[:, cols] + s * o).astype(BF)
        g = cot[:, cols].astype(F32)
        if with_delta:
            delta_out[:, cols] = (g * s).astype(BF)
            delta_gate[:, cols] = (g * o * s * (1.0 - s)).astype(BF)
        else:
            delta_out[:, cols] = s.astype(BF)
            delta_gate[:, cols] = (o * s * (1.0 - s)).astype(BF)
        return 0
    lax.fori_loop(0, width // tile, out_tile, 0)
    save(result)
    save(delta_out)
    save(delta_gate)
    for i, c in enumerate(saves):
        if i != 5:
            c.wait()

def forward(rows, with_delta, same_s, same, h, p, cot):
    (g1, b1, fade, bonus, mk, mv, mr, wk, wv, wr, wo, g2, b2, ck, cr, fk, fr, fv) = p
    tokens, width = h.shape
    ff = fk.shape[1]
    vm = pl.BlockSpec(memory_space=pltpu.VMEM)
    hbm = pl.BlockSpec(memory_space=pl.ANY)
    slabs = tokens * width // LANES
    outs = [((tokens, width), BF)] * 3 + [((slabs, LANES), F32)] * 2 + [((tokens, width), F32), ((tokens, width), BF), ((tokens, width), F32)]
    outs += [((tokens, width), BF)] * 2 + [((tokens, ff), BF)] * 2 + [((tokens, width), BF)] * 3
    outs = outs[:14] if False else outs
    wide, wide32, step32 = pltpu.VMEM((tokens, width), BF), pltpu.VMEM((tokens, width), F32), pltpu.VMEM((slabs, LANES), F32)
    stat = pltpu.VMEM((tokens, LANES), F32)
    square = pltpu.VMEM((width, width), BF)
    big = pltpu.VMEM((tokens, ff), BF)
    scratch = [square] * 4 + [pltpu.VMEM((width, ff), BF), square, pltpu.VMEM((ff, width), BF), stat, stat] + [wide] * 3
    scratch += [step32] * 3 + [wide32, wide, wide32, wide, wide, big, big, wide, wide, wide]
    scratch += [pltpu.SemaphoreType.DMA((7,)), pltpu.SemaphoreType.DMA((len(outs),))]
    return pl.pallas_call(
        functools.partial(forward_kernel, rows, with_delta),
        out_shape=tuple(jax.ShapeDtypeStruct(*o) for o in outs),
        in_specs=[pl.BlockSpec(memory_space=pltpu.SMEM)] + [vm] * 14 + [hbm] * 7,
        out_specs=(hbm,) * len(outs),
        scratch_shapes=scratch,
        compiler_params=pltpu.CompilerParams(vmem_limit_bytes=60 << 20),
        cost_estimate=pl.CostEstimate(flops=90000000000, bytes_accessed=261000000, transcendentals=0),
        name="forward",
    )(same_s, same, h, g1, b1, fade, bonus, mk, mv, mr, g2, b2, ck, cr, cot, wk, wv, wr, wo, fk, fr, fv)

def norm_backward(source, mean, scale, same, gain, bias, factors, grads, residual, targets, sums, first, second, tokens, width):
    first[...] = jnp.zeros_like(first)
    second[...] = jnp.zeros_like(second)
    def gather(c, _):
        cols = lanes(c)
        hat = (source[:, cols].astype(F32) - mean[...]) * scale[...]
        g = gain[:, cols].astype(F32)
        z = hat * g + bias[:, cols].astype(F32)
        step_up = z - pltpu.roll(z, 1, 0) * same[...]
        straight = jnp.zeros_like(z)
        total = jnp.zeros_like(z)
        for i, (factor, grad) in enumerate(zip(factors, grads)):
            d = grad[:, cols]
            f = factor[:, cols].astype(F32)
            sums[2 + i:3 + i, cols] = jnp.sum(d * step_up, axis=0, keepdims=True)
            straight = straight + d * f
            total = total + d
        dz = straight + pltpu.roll((total - straight) * same[...], tokens - 1, 0)
        sums[0:1, cols] = jnp.sum(dz * hat, axis=0, keepdims=True)
        sums[1:2, cols] = jnp.sum(dz, axis=0, keepdims=True)
        dhat = dz * g
        grads[0][:, cols] = dhat
        first[...] += dhat
        second[...] += dhat * hat
        return 0
    lax.fori_loop(0, width // LANES, gather, 0)
    for ref in (first, second):
        ref[...] = jnp.broadcast_to(jnp.sum(ref[...], axis=1, keepdims=True) * (1.0 / width), ref.shape)
    def finish(c, _):
        cols = lanes(c)
        hat = (source[:, cols].astype(F32) - mean[...]) * scale[...]
        out = residual[:, cols].astype(F32) + scale[...] * (grads[0][:, cols] - first[...] - hat * second[...])
        for t in targets:
            t[:, cols] = out.astype(t.dtype)
        return 0
    lax.fori_loop(0, width // LANES, finish, 0)

def channel_kernel(times, *refs):
    (same, factor_out, factor_gate, g, g2, b2, ck, cr, rect_in, middle_in, fv_in, fk_in, fr_in) = refs[:13]
    n_out = 6
    outs = refs[13:13 + n_out]
    (fv, fk, fr, rect, middle, delta_out, delta_gate, delta_pre, dh, dg, mean, scale, first, second, delta, branch, sums, in_sems, out_sems) = refs[13 + n_out:]
    tokens, width = g.shape
    ff = rect.shape[1]
    tile = 512
    chunks = ff // tile
    first_loads = []
    for j in range(chunks):
        span = slice(j * tile, (j + 1) * tile)
        first_loads += [(fv_in.at[span, :], fv.at[span, :]), (rect_in.at[:, span], rect.at[:, span])]
    loads = fetch(first_loads + [(fr_in, fr), (fk_in, fk), (middle_in, middle)], in_sems)
    saves = []
    def save(source, i):
        saves.append(pltpu.make_async_copy(source, outs[i], out_sems.at[i]))
        saves[-1].start()
    def cols_of(j):
        return pl.ds(pl.multiple_of(j * tile, tile), tile)
    if times:
        def scale_tile(j, _):
            cols = lanes(j)
            x = g[:, cols].astype(F32)
            delta_out[:, cols] = (x * factor_out[:, cols].astype(F32)).astype(BF)
            delta_gate[:, cols] = (x * factor_gate[:, cols].astype(F32)).astype(BF)
            return 0
        lax.fori_loop(0, width // LANES, scale_tile, 0)
        left_out, left_gate = delta_out, delta_gate
    else:
        left_out, left_gate = factor_out, factor_gate
    def pre_tile(j, _):
        cols = cols_of(j)
        pltpu.make_async_copy(fv_in.at[cols, :], fv.at[cols, :], in_sems.at[2 * j]).wait()
        pltpu.make_async_copy(rect_in.at[:, cols], rect.at[:, cols], in_sems.at[2 * j + 1]).wait()
        d = dot_nt(left_out[...], fv[cols, :])
        delta_pre[:, cols] = (d * (2.0 * rect[:, cols].astype(F32))).astype(BF)
        return 0
    lax.fori_loop(0, ff // tile, pre_tile, 0)
    save(delta_pre, 0)
    if times:
        save(delta_out, 4)
        save(delta_gate, 5)
    loads[-1].wait()
    statistics(middle, mean, scale, tokens, width)
    loads[-2].wait()
    loads[-3].wait()
    def hidden_tile(j, _):
        cols = cols_of(j)
        dh[:, cols] = dot_nt(delta_pre[...], fk[cols, :])
        dg[:, cols] = dot_nt(left_gate[...], fr[cols, :])
        return 0
    lax.fori_loop(0, width // tile, hidden_tile, 0)
    norm_backward(middle, mean, scale, same, g2, b2, (ck, cr), (dh, dg), g, (delta, branch), sums, first, second, tokens, width)
    save(delta, 1)
    save(branch, 2)
    save(sums, 3)
    for c in saves:
        c.wait()

def channel(times, same, factor_out, factor_gate, g, p, rect, middle):
    (g1, b1, fade, bonus, mk, mv, mr, wk, wv, wr, wo, g2, b2, ck, cr, fk, fr, fv) = p
    tokens, width = g.shape
    ff = fk.shape[1]
    vm = pl.BlockSpec(memory_space=pltpu.VMEM)
    hbm = pl.BlockSpec(memory_space=pl.ANY)
    outs = [((tokens, ff), BF), ((tokens, width), F32), ((tokens, width), BF), ((8, width), F32)]
    outs += [((tokens, width), BF)] * 2 if times else [((16, LANES), BF)] * 2
    wide, wide32 = pltpu.VMEM((tokens, width), BF), pltpu.VMEM((tokens, width), F32)
    stat = pltpu.VMEM((tokens, LANES), F32)
    big = pltpu.VMEM((tokens, ff), BF)
    scratch = [pltpu.VMEM((ff, width), BF), pltpu.VMEM((width, ff), BF), pltpu.VMEM((width, width), BF), big, wide32, wide, wide, big, wide32, wide32]
    scratch += [stat] * 4 + [wide32, wide, pltpu.VMEM((8, width), F32), pltpu.SemaphoreType.DMA((2 * ff // 512 + 3,)), pltpu.SemaphoreType.DMA((6,))]
    return pl.pallas_call(
        functools.partial(channel_kernel, times),
        out_shape=tuple(jax.ShapeDtypeStruct(*o) for o in outs),
        in_specs=[vm] * 8 + [hbm] * 5,
        out_specs=(hbm,) * 6,
        scratch_shapes=scratch,
        compiler_params=pltpu.CompilerParams(vmem_limit_bytes=60 << 20),
        cost_estimate=pl.CostEstimate(flops=75000000000, bytes_accessed=217500000, transcendentals=0),
        name="channel",
    )(same, factor_out, factor_gate, g, g2, b2, ck, cr, rect, middle, fv, fk, fr)

def time_kernel(rows, *refs):
    (same_s, same, branch, h, g1, b1, fade, bonus, mk, mv, mr, wo_in, gate_in, ks_in, vs_in, wk_in, wv_in, wr_in, delta_in) = refs[:19]
    n_out = 5
    outs = refs[19:19 + n_out]
    (wo, gate, ks, vs, wk, wv, wr, delta, dm, gs, ys, tops, bottoms, dk, dv, dr, ik, iv, ir, mean, scale, first, second, state, sums, in_sems, out_sems) = refs[19 + n_out:]
    tokens, width = h.shape
    each = tokens // rows
    parts = width // LANES
    tile = 512
    loads = fetch([(wo_in, wo), (gate_in, gate), (ks_in, ks), (vs_in, vs), (wk_in, wk), (wv_in, wv), (wr_in, wr), (delta_in, delta)], in_sems)
    saves = []
    def save(source, i):
        saves.append(pltpu.make_async_copy(source, outs[i], out_sems.at[i]))
        saves[-1].start()
    def cols_of(j):
        return pl.ds(pl.multiple_of(j * tile, tile), tile)
    loads[0].wait()
    loads[1].wait()
    def mixed_tile(j, _):
        cols = cols_of(j)
        d = dot_nt(branch[...], wo[cols, :])
        dm[:, cols] = d
        e = d * gate[:, cols]
        for row in range(rows):
            for c in range(tile // LANES):
                gs[pl.ds(row * each * parts + j * (tile // LANES) + c, each, stride=parts), :] = e[row * each:(row + 1) * each, c * LANES:(c + 1) * LANES]
        return 0
    lax.fori_loop(0, width // tile, mixed_tile, 0)
    statistics(h, mean, scale, tokens, width)
    loads[2].wait()
    loads[3].wait()
    rate = jnp.exp(fade[...])
    decay = jnp.exp(-rate)
    extra = bonus[...]
    def step(t, carry):
        following = []
        for row in range(rows):
            here = pl.ds(pl.multiple_of((row * each + t) * parts, parts), parts)
            m = same_s[row, t]
            top, bottom = carry[2 * row] * m, carry[2 * row + 1] * m
            tops[here, :] = top
            bottoms[here, :] = bottom
            k, v = ks[here, :], vs[here, :]
            ek, now = jnp.exp(k), jnp.exp(extra + k)
            inverse = 1.0 / (bottom + now)
            ys[here, :] = (top + now * v) * inverse
            gs[here, :] = gs[here, :] * inverse
            following += [decay * top + ek * v, decay * bottom + ek]
        return tuple(following)
    zero = jnp.zeros(decay.shape, F32)
    lax.fori_loop(0, each, step, (zero,) * (2 * rows), unroll=4)
    def back(i, carry):
        t = each - 1 - i
        dw, du = carry[:2]
        following = []
        for row in range(rows):
            here = pl.ds(pl.multiple_of((row * each + t) * parts, parts), parts)
            a, b = carry[2 + 2 * row], carry[3 + 2 * row]
            k, v = ks[here, :], vs[here, :]
            ek, now = jnp.exp(k), jnp.exp(extra + k)
            ga = gs[here, :]
            gb = -ga * ys[here, :]
            q = now * (v * ga + gb)
            ks[here, :] = ek * (v * a + b) + q
            vs[here, :] = ek * a + now * ga
            du = du + q
            dw = dw + (a * tops[here, :] + b * bottoms[here, :])
            m = same_s[row, t]
            following += [(ga + decay * a) * m, (gb + decay * b) * m]
        return (dw, du, *following)
    done = lax.fori_loop(0, each, back, (zero,) * (2 + 2 * rows), unroll=4)
    dfade = -done[0] * decay * rate
    for c in range(parts):
        sums[5:6, c * LANES:(c + 1) * LANES] = dfade[c:c + 1, :]
        sums[6:7, c * LANES:(c + 1) * LANES] = done[1][c:c + 1, :]
    for row in range(rows):
        def out_step(c, _, row=row):
            span = slice(row * each, (row + 1) * each)
            cols = lanes(c)
            at = pl.ds(row * each * parts + c, each, stride=parts)
            dk[span, cols] = ks[at, :].astype(BF)
            dv[span, cols] = vs[at, :].astype(BF)
            s = gate[span, cols]
            dr[span, cols] = (dm[span, cols] * ys[at, :] * s * (1.0 - s)).astype(BF)
            return 0
        lax.fori_loop(0, parts, out_step, 0)
    for i, z in enumerate((dk, dv, dr)):
        save(z, i)
    for i in (4, 5, 6):
        loads[i].wait()
    def in_tile(j, _):
        cols = cols_of(j)
        ik[:, cols] = dot_nt(dk[...], wk[cols, :])
        iv[:, cols] = dot_nt(dv[...], wv[cols, :])
        ir[:, cols] = dot_nt(dr[...], wr[cols, :])
        return 0
    lax.fori_loop(0, width // tile, in_tile, 0)
    loads[7].wait()
    norm_backward(h, mean, scale, same, g1, b1, (mk, mv, mr), (ik, iv, ir), delta, (state,), sums, first, second, tokens, width)
    save(state, 3)
    save(sums, 4)
    for c in saves:
        c.wait()

def time_mix(rows, dtype, same_s, same, branch, delta, h, p, gate, ks, vs):
    (g1, b1, fade, bonus, mk, mv, mr, wk, wv, wr, wo, g2, b2, ck, cr, fk, fr, fv) = p
    tokens, width = h.shape
    vm = pl.BlockSpec(memory_space=pltpu.VMEM)
    hbm = pl.BlockSpec(memory_space=pl.ANY)
    outs = [((tokens, width), BF)] * 3 + [((tokens, width), dtype), ((8, width), F32)]
    wide, wide32 = pltpu.VMEM((tokens, width), BF), pltpu.VMEM((tokens, width), F32)
    step32 = pltpu.VMEM(ks.shape, F32)
    stat = pltpu.VMEM((tokens, LANES), F32)
    square = pltpu.VMEM((width, width), BF)
    scratch = [square, wide32, step32, step32, square, square, square, wide32, wide32] + [step32] * 4 + [wide] * 3 + [wide32] * 3 + [stat] * 4
    scratch += [pltpu.VMEM((tokens, width), dtype), pltpu.VMEM((8, width), F32), pltpu.SemaphoreType.DMA((8,)), pltpu.SemaphoreType.DMA((5,))]
    return pl.pallas_call(
        functools.partial(time_kernel, rows),
        out_shape=tuple(jax.ShapeDtypeStruct(*o) for o in outs),
        in_specs=[pl.BlockSpec(memory_space=pltpu.SMEM)] + [vm] * 10 + [hbm] * 8,
        out_specs=(hbm,) * 5,
        scratch_shapes=scratch,
        compiler_params=pltpu.CompilerParams(vmem_limit_bytes=60 << 20),
        cost_estimate=pl.CostEstimate(flops=87000000000, bytes_accessed=252300000, transcendentals=0),
        name="time_mix",
    )(same_s, same, branch, h, g1, b1, fade, bonus, mk, mv, mr, wo, gate, ks, vs, wk, wv, wr, delta)


UNIT = 1024


def starts(parts):
    return [sum(c for c, _ in parts[:i]) for i in range(len(parts))]


def terms_kernel(count, parts, shapes, with_sums, *refs):
    bits, refs = refs[0], refs[1:]
    n, np_ = len(shapes), len(parts)
    left_in, right_in, refs = refs[:n], refs[n:2 * n], refs[2 * n:]
    if with_sums:
        early, late, *refs = refs
    outs, refs = refs[:2 * np_], refs[2 * np_:]
    lefts, rights, refs = refs[:n], refs[n:2 * n], refs[2 * n:]
    bufs, (in_sems, out_sems) = refs[:np_], refs[np_:]
    sends, keeps = outs[::2], outs[1::2]
    tile = 256
    columns = starts(parts)

    def place(order, d):
        bit = [(d >> b) & 1 if isinstance(d, int) else lax.rem(lax.div(d, 1 << b), 2) for b in order]
        return bit[0] ^ bits[order[0]], bit[1] * 4 + bit[2] * 2 + bit[3]

    loads = []
    for i in range(n):
        loads.append(pltpu.make_async_copy(right_in[i], rights[i], in_sems.at[2 * i]))
        loads.append(pltpu.make_async_copy(left_in[i], lefts[i], in_sems.at[2 * i + 1]))
    for c in loads:
        c.start()
    waits = []
    base = 0
    for m, ((kin, width), left, right) in enumerate(zip(shapes, lefts, rights)):
        rows = kin // count
        per = max(tile // rows, 1)
        loads[2 * m].wait()
        loads[2 * m + 1].wait()

        def step(j, _, left=left, right=right, rows=rows, per=per, width=width, base=base):
            lhs = left[:, pl.ds(pl.multiple_of(j * tile, tile), tile)]
            for q in range(width // UNIT):
                for i, (cols, order) in enumerate(parts):
                    at = q * UNIT + columns[i]
                    res = lax.dot_general(lhs, right[:, at:at + cols], (((0,), (0,)), ((), ())), preferred_element_type=F32).astype(BF)
                    for s in range(per):
                        relative, index = place(order, j * per + s)
                        bufs[i][relative, index, base + q * rows:base + (q + 1) * rows, :] = res[s * rows:(s + 1) * rows]
                        if rows == tile:
                            source = bufs[i].at[relative, index]
                            for r, target in ((1, sends[i]), (0, keeps[i])):
                                @pl.when(relative == r)
                                def _(source=source, target=target, index=index, i=i):
                                    pltpu.make_async_copy(source, target.at[index], out_sems.at[i, j]).start()
            return 0

        lax.fori_loop(0, kin // tile, step, 0)
        span = rows * (width // UNIT)
        for i in range(np_):
            if rows == tile:
                for j in range(kin // tile):
                    waits.append(pltpu.make_async_copy(bufs[i].at[0, 0], keeps[i].at[0], out_sems.at[i, j]))
            else:
                for r, target in ((1, sends[i]), (0, keeps[i])):
                    c = pltpu.make_async_copy(bufs[i].at[r, :, base:base + span, :], target.at[:, base:base + span, :], out_sems.at[i, 2 * m + r])
                    c.start()
                    waits.append(c)
        base += span
    if with_sums:
        share = early.shape[1] // count
        both = jnp.concatenate([early[...], late[...]], axis=0)
        for buf in bufs:
            buf[:, :, base:base + 16, :] = jnp.zeros(buf.shape[:2] + (16, buf.shape[3]), BF)
        for d in range(count):
            column = d * share // LANES * LANES
            piece = both[:, column:column + LANES]
            if d * share - column:
                piece = pltpu.roll(piece, LANES - (d * share - column), 1)
            relative, index = place(parts[0][1], d)
            bufs[0][relative, index, base:base + 16, 0:LANES] = piece.astype(BF)
        for i in range(np_):
            for r, target in ((1, sends[i]), (0, keeps[i])):
                c = pltpu.make_async_copy(bufs[i].at[r, :, base:base + 16, :], target.at[:, base:base + 16, :], out_sems.at[i, 2 * n + r])
                c.start()
                waits.append(c)
    for c in waits:
        c.wait()


def terms(bits, parts, pairs, sums=()):
    count = 16
    lefts, rights = zip(*pairs)
    shapes = tuple((a.shape[1], b.shape[1]) for a, b in pairs)
    tokens = lefts[0].shape[0]
    rows = sum(kin // count * (width // UNIT) for kin, width in shapes) + (16 if sums else 0)
    outs, bufs = [], []
    for cols, _ in parts:
        outs += [jax.ShapeDtypeStruct((count // 2, rows, cols), BF)] * 2
        bufs.append(pltpu.VMEM((2, count // 2, rows, cols), BF))
    flops = sum(2 * tokens * kin * width for kin, width in shapes)
    result = pl.pallas_call(
        functools.partial(terms_kernel, count, parts, shapes, bool(sums)),
        out_shape=tuple(outs),
        in_specs=[SM] + [HBM] * (2 * len(shapes)) + [VM] * len(sums),
        out_specs=(HBM,) * len(outs),
        scratch_shapes=[pltpu.VMEM(x.shape, BF) for x in (*lefts, *rights)]
        + bufs + [pltpu.SemaphoreType.DMA((2 * len(shapes),)), pltpu.SemaphoreType.DMA((len(parts), 16))],
        compiler_params=pltpu.CompilerParams(vmem_limit_bytes=56 << 20),
        cost_estimate=pl.CostEstimate(flops=39000000000, bytes_accessed=113100000, transcendentals=0),
        name="terms",
    )(bits, *lefts, *rights, *sums)
    return list(zip(result[::2], result[1::2]))


def swap(block, bit):
    count = lax.axis_size("dp")
    return lax.ppermute(block, "dp", [(i, i ^ (1 << bit)) for i in range(count)])


def summed(kept, came, dtype=BF):
    return (kept.astype(F32) + came.astype(F32)).astype(dtype)


def advance_kernel(bits, kept_go, came_go, kept_stay, came_stay, send, keep):
    send[...] = summed(kept_go[...], came_go[...])
    keep[...] = summed(kept_stay[...], came_stay[...])


def advance(bits, kept, came, bit):
    lead, rows, cols = kept.shape
    half = lead // 2
    block = rows // 2 if rows % 32 == 0 else rows
    go = pl.BlockSpec((1, block, cols), lambda g, i, b: ((1 - b[bit]) * half + g, i, 0))
    stay = pl.BlockSpec((1, block, cols), lambda g, i, b: (b[bit] * half + g, i, 0))
    out = pl.BlockSpec((1, block, cols), lambda g, i, b: (g, i, 0))
    return pl.pallas_call(
        advance_kernel,
        out_shape=(jax.ShapeDtypeStruct((half, rows, cols), BF),) * 2,
        grid_spec=pltpu.PrefetchScalarGridSpec(
            num_scalar_prefetch=1, grid=(half, rows // block), in_specs=[go, go, stay, stay], out_specs=(out, out)
        ),
        compiler_params=pltpu.CompilerParams(vmem_limit_bytes=30 << 20),
        cost_estimate=pl.CostEstimate(flops=9000000000, bytes_accessed=26100000, transcendentals=0),
        name="advance",
    )(bits, kept, came, kept, came)


def final_kernel(pieces, parts, *refs):
    n = len(parts)
    ins, outs = refs[:2 * n], refs[2 * n:]
    for (row, rows, blocks, columns), out in zip(pieces, outs):
        for q in range(blocks):
            span = slice(row + q * rows, row + (q + 1) * rows)
            if columns < UNIT:
                out[...] = summed(ins[0][0, span, 0:LANES], ins[1][0, span, 0:LANES], F32)[:, :columns]
                continue
            for i, at in enumerate(starts(parts)):
                out[:, q * UNIT + at:q * UNIT + at + parts[i][0]] = summed(ins[2 * i][0, span, :], ins[2 * i + 1][0, span, :], F32)


def final(parts, pieces, arrays):
    size = sum(a.size for a in arrays)
    return pl.pallas_call(
        functools.partial(final_kernel, pieces, parts),
        out_shape=tuple(jax.ShapeDtypeStruct((rows, blocks * columns), F32) for row, rows, blocks, columns in pieces),
        in_specs=[VM] * len(arrays),
        out_specs=(VM,) * len(pieces),
        compiler_params=pltpu.CompilerParams(vmem_limit_bytes=40 << 20),
        cost_estimate=pl.CostEstimate(flops=4500000000, bytes_accessed=13050000, transcendentals=0),
        name="final",
    )(*arrays)


def after(value, *earlier):
    return lax.optimization_barrier((value, earlier))[0]


class Line:
    def __init__(self, bits, plan, pieces):
        self.bits, self.plan, self.pieces, self.token, self.flight, self.sums = bits, plan, pieces, None, {}, {}

    def tie(self, value):
        return value if self.token is None else after(value, self.token)

    def open(self, group, pairs, sums=()):
        pairs = ((self.tie(pairs[0][0]), pairs[0][1]),) + tuple(pairs[1:])
        found = terms(self.bits, self.plan[group], pairs, sums)
        self.token = found
        for i, (send, keep) in enumerate(found):
            self.flight[group, i] = keep, swap(send, self.plan[group][i][1][0])

    def serve(self, steps):
        for group, i, stage in steps:
            parts = self.plan[group]
            if stage < 4:
                kept, came = self.tie(self.flight[group, i])
                send, keep = advance(self.bits, kept, came, parts[i][1][stage])
                self.token = send, keep
                self.flight[group, i] = keep, swap(send, parts[i][1][stage])
            else:
                self.sums[group, i] = self.flight.pop((group, i))
                if all((group, k) in self.sums for k in range(len(parts))):
                    arrays = [a for k in range(len(parts)) for a in self.sums[group, k]]
                    arrays[0] = self.tie(arrays[0])
                    self.sums[group] = final(parts, self.pieces[group], arrays)
                    self.token = self.sums[group][0]


def halving(left, right=None):
    count = lax.axis_size("dp")
    bits = count.bit_length() - 1
    me = lax.axis_index("dp")
    if right is not None:
        left = lax.dot_general(left, right, (((0,), (0,)), ((), ())), preferred_element_type=F32).astype(BF)
    current = left.reshape((2,) * bits + (left.shape[0] // count, left.shape[1]))
    for bit in range(bits):
        axis = bits - 1 - bit
        mine = (me >> bit) & 1
        send = lax.dynamic_index_in_dim(current, 1 - mine, axis, keepdims=False)
        keep = lax.dynamic_index_in_dim(current, mine, axis, keepdims=False)
        current = summed(keep, swap(send, bit), BF if bit + 1 < bits else F32)
    return current


def unwritten(function, *args):
    shapes, tree = jax.tree.flatten(jax.eval_shape(function, *args))
    outs = pl.pallas_call(
        lambda *refs: None, out_shape=tuple(shapes), out_specs=(HBM,) * len(shapes), name="unwritten"
    )()
    return jax.tree.unflatten(tree, outs)


VECTORS = (0, 1, 5, 6, 2, 3, 4, 8, 9, 10, 11)
PARTS_0 = dict(
    a=((512, (0, 1, 2, 3)), (512, (2, 3, 1, 0))),
    b=((640, (0, 1, 2, 3)), (384, (0, 2, 1, 3))),
    e=((512, (0, 1, 2, 3)), (512, (1, 0, 2, 3))),
)
PARTS_1 = dict(
    a=((640, (2, 1, 3, 0)), (384, (2, 3, 1, 0))),
    b=((384, (2, 1, 3, 0)), (640, (1, 2, 0, 3))),
    e=((512, (0, 2, 3, 1)), (512, (1, 0, 2, 3))),
)
STEPS_0 = (
    (),
    (('a', 0, 1), ('a', 1, 1)),
    (('b', 0, 1), ('a', 0, 2), ('a', 1, 2), ('b', 1, 1), ('a', 0, 3), ('e', 1, 1), ('b', 1, 2), ('b', 0, 2), ('a', 1, 3), ('a', 0, 4), ('e', 0, 1), ('b', 1, 3), ('e', 1, 2), ('a', 1, 4), ('b', 0, 3), ('e', 0, 2), ('b', 1, 4), ('e', 1, 3), ('e', 0, 3), ('b', 0, 4), ('e', 1, 4), ('e', 0, 4)),
)
STEPS_1 = (
    (),
    (('a', 0, 1), ('a', 1, 1)),
    (),
    (('a', 0, 2), ('a', 1, 2), ('e', 0, 1), ('b', 0, 1), ('b', 1, 1), ('a', 0, 3), ('e', 0, 2), ('e', 1, 1), ('a', 1, 3), ('b', 1, 2), ('b', 0, 2), ('e', 0, 3), ('a', 0, 4), ('e', 1, 2), ('a', 1, 4), ('b', 0, 3), ('b', 1, 3), ('e', 1, 3), ('e', 0, 4), ('b', 1, 4), ('e', 1, 4), ('b', 0, 4)),
)


def local(entry_pair, labels, *params):
    count = lax.axis_size("dp")
    section = lax.axis_index("section")
    rows, each, width = entry_pair.shape[1:]
    own = entry_pair.reshape(rows * each, width)
    share = width // count
    p = [e if e.ndim == 2 else e[0] for e in params]
    ff = p[15].shape[1]
    for i in (2, 3):
        p[i] = p[i].reshape(width // LANES, LANES).astype(F32)
    first = jnp.zeros((rows, 1), F32)
    same_s = jnp.concatenate([first, (labels[:, 1:] == labels[:, :-1]).astype(F32)], axis=1)
    same = jnp.broadcast_to(same_s.reshape(rows * each, 1), (rows * each, LANES))
    fast = count == 16 and width == UNIT
    me = lax.axis_index("dp")
    bits = jnp.stack([(me >> i) & 1 for i in range(4)])
    wide = ff // width
    pieces = dict(
        a=((0, ff // count, 1, width),),
        b=((0, share, wide, width), (share * wide, share, 1, width), (share * (wide + 1), share, 1, width)),
        e=tuple((i * share, share, 1, width) for i in range(3)) + tuple((3 * share + i, 1, 1, share) for i in VECTORS),
    )

    def plain_rest(pairs, sums):
        together = jnp.concatenate(sums).astype(BF).reshape(16, count, share).transpose(1, 0, 2).reshape(count * 16, share)
        vectors = halving(together)
        return tuple(halving(*pair) for pair in pairs) + tuple(vectors[i:i + 1] for i in VECTORS)

    def start():
        return forward(rows, False, same_s, same, own, p, own)

    def middle_part(received):
        kept = forward(rows, True, same_s, same, received, p, own)
        (key_in, value_in, recept_in, ks, vs, gate, mixed, middle, hidden_in, gate_in, rect, act, result, delta_out, delta_gate) = kept
        line = Line(bits, PARTS_1, pieces)
        if fast:
            line.open("a", ((act, delta_out),))
        delta_pre, delta, branch, late, _, _ = channel(False, same, delta_out, delta_gate, line.tie(own), p, rect, middle)
        line.token = branch
        if fast:
            line.serve(STEPS_1[0])
        dk, dv, dr, state, early = time_mix(rows, BF, same_s, same, line.tie(branch), delta, received, p, gate, ks, vs)
        key_pairs = ((hidden_in, delta_pre), (gate_in, delta_gate), (mixed, branch))
        begun = list(line.flight.values()) if fast else (act, delta_out)
        return state, result, begun, (early, late), key_pairs, ((key_in, dk), (value_in, dv), (recept_in, dr))

    def end_first(received, kept):
        (key_in, value_in, recept_in, ks, vs, gate, mixed, middle, hidden_in, gate_in, rect, act, result, factor_out, factor_gate) = kept
        line = Line(bits, PARTS_0, pieces)
        if fast:
            line.open("a", ((act, (received.astype(F32) * factor_out.astype(F32)).astype(BF)),))
        g = line.tie(received)
        delta_pre, delta, branch, late, delta_out, delta_gate = channel(True, same, factor_out, factor_gate, g, p, rect, middle)
        key_pairs = ((hidden_in, delta_pre), (gate_in, delta_gate), (mixed, branch))
        line.token = branch
        if fast:
            line.serve(STEPS_0[0])
            line.open("b", key_pairs)
            line.serve(STEPS_0[1])
        dk, dv, dr, state, early = time_mix(rows, F32, same_s, same, line.tie(branch), delta, own, p, gate, ks, vs)
        rest_pairs = ((key_in, dk), (value_in, dv), (recept_in, dr))
        if not fast:
            return state, (halving(act, delta_out),), tuple(halving(*pair) for pair in key_pairs), plain_rest(rest_pairs, (early, late))
        line.token = state
        line.open("e", rest_pairs, (early, late))
        line.serve(STEPS_0[2])
        return state, line.sums["a"], line.sums["b"], line.sums["e"]

    def end_second(result, begun, sums, key_pairs, rest_pairs):
        if not fast:
            return result.astype(F32), (halving(*begun),), tuple(halving(*pair) for pair in key_pairs), plain_rest(rest_pairs, sums)
        line = Line(bits, PARTS_1, pieces)
        line.flight = {("a", i): pair for i, pair in enumerate(begun)}
        line.serve(STEPS_1[1])
        line.open("b", key_pairs)
        line.serve(STEPS_1[2])
        line.open("e", rest_pairs, sums)
        line.serve(STEPS_1[3])
        return result.astype(F32), line.sums["a"], line.sums["b"], line.sums["e"]

    kept = lax.cond(section == 0, start, lambda: unwritten(start))
    received = lax.ppermute(kept[12], "section", [(0, 1)])
    delta, *pending = lax.cond(section == 1, middle_part, lambda r: unwritten(middle_part, r), received)
    received = lax.ppermute(delta, "section", [(1, 0)])
    ends, (value_sum,), (key_sum, gate_sum, exit_sum), rest = lax.cond(
        section == 0, lambda r, k, q: end_first(r, k), lambda r, k, q: end_second(*q), received, kept, pending
    )
    ends = ends.reshape(rows, each, width)
    everything = (ends, *(z[0] for z in rest[3:10]), *rest[:3], exit_sum, *(z[0] for z in rest[10:14]), key_sum, gate_sum, value_sum)
    return tuple(e[None] for e in everything)


def solution(mesh):
    vec, mat = P("section", None), P("section", None, None)
    in_specs = (P("section", "dp", None, None), P("dp", None)) + (vec,) * 7 + (mat,) * 4 + (vec,) * 4 + (mat,) * 3
    vec, mat = P("section", "dp"), P("section", "dp", None)
    out_specs = (P("section", "dp", None, None),) + (vec,) * 7 + (mat,) * 4 + (vec,) * 4 + (mat,) * 3
    return jax.shard_map(local, mesh=mesh, in_specs=in_specs, out_specs=out_specs, check_vma=False)
```

time: 755 us -> 376 us (0.50)
  waiting for transfers between devices: 360 us -> 161 us
  Pallas kernels: 19.3 us -> 161 us
  local copies, waits for them, and re-layouts: 125 us -> 2.23 us
  matrix products: 92.7 us -> 0 us
  other arithmetic: 77 us -> 5.38 us
  starting transfers between devices: 64.1 us -> 32.6 us
    ppermute x62 -> x26, waiting for transfers between devices: 360 us -> 161 us  [the longest x1 97.5 us: local(): received = lax.ppermute(delta, 'section', [(1, 0)])]
    pallas_call x2 -> x28, Pallas kernels: 19.3 us -> 161 us  [the longest x3 38.6 us: terms(): pl.pallas_call(functools.partial(terms_kernel, count, parts, shapes, bool...]
    dot_general x28 -> x0, matrix products: 92.7 us -> none  [the longest x14 38.1 us: outer_product(): lax.dot_general(left, right, (((0, 1), (0, 1)), ((), ())), preferred_elem...]
    cond x109 -> x56, local copies, waits for them, and re-layouts: 50.7 us -> 2.1 us
    convert_element_type x58 -> x3, other arithmetic: 43.3 us -> 4.39 us  [the longest x1 3.01 us: end_first(): (received.astype(F32) * factor_out.astype(F32)).astype(BF)]
    ppermute x62 -> x26, starting transfers between devices: 64.1 us -> 32.6 us  [the longest x24 30 us: swap(): return lax.ppermute(block, 'dp', [(i, i ^ 1 << bit) for i in range(count)])]
    squeeze x56 -> x0, local copies, waits for them, and re-layouts: 29.4 us -> none  [halving(): send = lax.dynamic_index_in_dim(current, 1 - mine, axis, keepdims=False)]
    another operation x17 -> x0, local copies, waits for them, and re-layouts: 21.9 us -> none
  transfers between devices with their start and end apart: 62 -> 26, of which waited for: 47 -> 11; matrix products, arithmetic and copies ran while one was open for 8% -> 0% of each run, Pallas kernels for 0% -> 32%
where the time goes in v2:
time: 376 us; the launch traced here: 371 us
  Pallas kernels  161 us (43%)
  waiting for transfers between devices  161 us (43%)
  starting transfers between devices  32.6 us (9%)
  loops' own time  7.31 us (2%)
  other arithmetic  5.38 us (1%)
    ppermute x1, waiting for transfers between devices, local(): received = lax.ppermute(delta, 'section', [(1, 0)])  97.5 us
    ppermute x24, waiting for transfers between devices, swap(): return lax.ppermute(block, 'dp', [(i, i ^ 1 << bit) for i in range(count)])  61.1 us
    pallas_call x3, Pallas kernels, terms(): pl.pallas_call(functools.partial(terms_kernel, count, parts, shapes, bool...  38.6 us
    pallas_call x18, Pallas kernels, advance(): pl.pallas_call(advance_kernel, out_shape=(jax.ShapeDtypeStruct((half, row...  35 us
    pallas_call x1, Pallas kernels, forward(): pl.pallas_call(functools.partial(forward_kernel, rows, with_delta), out_s...  30.1 us
    ppermute x24, starting transfers between devices, swap(): return lax.ppermute(block, 'dp', [(i, i ^ 1 << bit) for i in range(count)])  30 us
    pallas_call x1, Pallas kernels, time_mix(): pl.pallas_call(functools.partial(time_kernel, rows), out_shape=tuple((jax...  29.5 us
    pallas_call x1, Pallas kernels, channel(): pl.pallas_call(functools.partial(channel_kernel, times), out_shape=tuple(...  24.5 us
  transfers between devices with their start and end apart: 26, of which 11 were waited for; matrix products, arithmetic and copies ran while one was open for 0% of the time, Pallas kernels for 32%

profile of v2, /device:TPU:0, one launch (start us, length us, event | category | flops | bytes accessed | tf_op | source)
XLA Modules:
  0.0 370.9 jit_solution(9176927287390013213)
XLA Ops:
  3.1 30.1 %conditional.3 = ((bf16[512,1024]{1,0:T(8,128)(2,1)}, bf16[512,1024]{1,0:T(8,128)(2,1)}, bf16[512,1024]{1,0:T(8,128)(2,1)}, f32[4096,128]{1,0:T(8,128)}, f32[409...) conditional(s32[]{:T(128)} %convert_element_type.30, () %tuple.83, ...), branch_computations={%region_0.0_spmd, %region_1.0_spmd} | conditional | flops 89999998976 | bytes 261000000 | solution.py:790
  3.1 30.1 %forward.2 = (bf16[512,1024]{1,0:T(8,128)(2,1)}, bf16[512,1024]{1,0:T(8,128)(2,1)}, bf16[512,1024]{1,0:T(8,128)(2,1)}, f32[4096,128]{1,0:T(8,128)}, f32[4096,128...) custom-call(f32[2,256]{1,0:T(2,128)S(1)} %get-tuple-element.204.refs, ...), custom_call_target="tpu_custom_call" | custom-call | flops 89999998976 | bytes 261000000 | tf_op jit(solution)/shard_map/cond/branch_1_fun/forward/pallas_call | solution.py:195
  36.8 6.6 %conditional.4 = ((bf16[512,1024]{1,0:T(8,128)(2,1)}, bf16[512,1024]{1,0:T(8,128)(2,1)}, bf16[8,256,640]{2,1,0:T(8,128)(2,1)}, bf16[8,256,640]{2,1,0:T(8,128)(2,...) conditional(s32[]{:T(128)} %convert_element_type.31, () %tuple.82, ...), branch_computations={%region_2.0_spmd, %region_3.0_spmd} | conditional | flops 290999959552 | bytes 877528704 | solution.py:792
  44.7 97.5 %collective-permute-done.49 = bf16[512,1024]{1,0:T(8,128)(2,1)} collective-permute-done((bf16[512,1024]{1,0:T(8,128)(2,1)}, bf16[512,1024]{1,0:T(8,128)(2,1)}, u32[]{:S(2)}, u32[]{:S(2)}) %collective-permute-start.49) | collective-permute-done | bytes 1048608 | tf_op jit(solution)/shard_map/ppermute | solution.py:793
  142.2 227.6 %conditional.5 = (f32[64,4096]{1,0:T(8,128)}, f32[64,1024]{1,0:T(8,128)}, f32[64,1024]{1,0:T(8,128)}, f32[64,1024]{1,0:T(8,128)}, f32[64,1024]{1,0:T(8,128)}, /*...) conditional(s32[]{:T(128)} %convert_element_type.30, ...), branch_computations={%region_4.0_spmd, %region_5.0_spmd} | conditional | flops 454501957632 | bytes 1512544896 | solution.py:794
  142.2 3.0 multiply_convert_fusion.refs_2_
  145.3 12.5 %terms.9 = (bf16[8,256,512]{2,1,0:T(8,128)(2,1)}, bf16[8,256,512]{2,1,0:T(8,128)(2,1)}, bf16[8,256,512]{2,1,0:T(8,128)(2,1)}, bf16[8,256,512]{2,1,0:T(8,128)(2,1)}) custom-call(s32[4]{0:T(128)} %copy-done.28, bf16[512,4096]{1,0:T(8,128)(2,1)} %get-tuple-element.404.refs_1_, bf16[512,1024]{1,0:T(8,128)(2,1)} %multiply_convert_fusion.refs_2_), custom_call_target="tpu_custom_call" | custom-call | flops 38999998464 | bytes 113100000 | tf_op jit(solution)/shard_map/cond/branch_1_fun/terms/pallas_call | solution.py:554
  161.1 24.5 %channel.3 = (bf16[512,4096]{1,0:T(8,128)(2,1)}, f32[512,1024]{1,0:T(8,128)}, bf16[512,1024]{1,0:T(8,128)(2,1)}, f32[8,1024]{1,0:T(8,128)}, bf16[512,1024]{1,0:T(8,128)(2,1)}, /*index=5*/bf16[512,1024]{1,0:T(8,128)(2,1)}) custom-call(f32[512,128]{1,0:T(8,128)S(1)} %copy-done.19, bf16[512,1024]{1,0:T(8,128)(2,1)S(1)} %copy-done.17, ...), custom_call_target="tpu_custom_call" | custom-call | flops 74999996416 | bytes 217500000 | tf_op jit(solution)/shard_map/cond/branch_1_fun/channel/pallas_call | solution.py:316
  185.6 15.6 %terms.10 = (bf16[8,384,640]{2,1,0:T(8,128)(2,1)}, bf16[8,384,640]{2,1,0:T(8,128)(2,1)}, bf16[8,384,384]{2,1,0:T(8,128)(2,1)}, bf16[8,384,384]{2,1,0:T(8,128)(2,1)}) custom-call(s32[4]{0:T(128)S(1)} %copy-done.29, bf16[512,1024]{1,0:T(8,128)(2,1)} %get-tuple-element.420.refs_1_, bf16[512,1024]{1,0:T(8,128)(2,1)} %get-tuple-element.421.refs_2_, ...), custom_call_target="tpu_custom_call" | custom-call | flops 38999998464 | bytes 113100000 | tf_op jit(solution)/shard_map/cond/branch_1_fun/terms/pallas_call | solution.py:554
  203.3 6.2 %advance.54 = (bf16[4,256,512]{2,1,0:T(8,128)(2,1)}, bf16[4,256,512]{2,1,0:T(8,128)(2,1)S(1)}) custom-call(s32[4]{0:T(128)S(1)} %copy-done.29, bf16[8,256,512]{2,1,0:T(8,128)(2,1)S(1)} %copy-done.5, bf16[8,256,512]{2,1,0:T(8,128)(2,1)} %collective-permute-done.26.came_go.came_stay, bf16[8,256,512]{2,1,0:T(8,128)(2,1)S(1)} %copy-done.5, ...), custom_call_target="tpu_custom_call" | custom-call | flops 8999999488 | bytes 26100000 | tf_op jit(solution)/shard_map/cond/branch_1_fun/advance/pallas_call | solution.py:589
  212.1 6.1 %advance.55 = (bf16[4,256,512]{2,1,0:T(8,128)(2,1)}, bf16[4,256,512]{2,1,0:T(8,128)(2,1)S(1)}) custom-call(s32[4]{0:T(128)S(1)} %copy-done.29, bf16[8,256,512]{2,1,0:T(8,128)(2,1)S(1)} %copy-done.4, bf16[8,256,512]{2,1,0:T(8,128)(2,1)} %collective-permute-done.25.came_go.came_stay, bf16[8,256,512]{2,1,0:T(8,128)(2,1)S(1)} %copy-done.4, ...), custom_call_target="tpu_custom_call" | custom-call | flops 8999999488 | bytes 26100000 | tf_op jit(solution)/shard_map/cond/branch_1_fun/advance/pallas_call | solution.py:589
  219.2 2.6 collective-permute-start.29
  221.8 29.5 %time_mix.3 = (bf16[512,1024]{1,0:T(8,128)(2,1)}, bf16[512,1024]{1,0:T(8,128)(2,1)}, bf16[512,1024]{1,0:T(8,128)(2,1)}, f32[512,1024]{1,0:T(8,128)}, f32[8,1024]{1,0:T(8,128)}) custom-call(f32[2,256]{1,0:T(2,128)S(1)} %copy-done.25, f32[512,128]{1,0:T(8,128)} %copy-done.18, bf16[512,1024]{1,0:T(8,128)(2,1)} %get-tuple-element.439.refs_6_.refs_2_, ...), custom_call_target="tpu_custom_call" | custom-call | flops 86999998464 | bytes 252300000 | tf_op jit(solution)/shard_map/cond/branch_1_fun/time_mix/pallas_call | solution.py:443
  251.4 10.4 %terms.11 = (bf16[8,208,512]{2,1,0:T(8,128)(2,1)}, bf16[8,208,512]{2,1,0:T(8,128)(2,1)}, bf16[8,208,512]{2,1,0:T(8,128)(2,1)}, bf16[8,208,512]{2,1,0:T(8,128)(2,1)}) custom-call(s32[4]{0:T(128)S(1)} %copy-done.29, bf16[512,1024]{1,0:T(8,128)(2,1)} %get-tuple-element.457.refs_1_, bf16[512,1024]{1,0:T(8,128)(2,1)} %get-tuple-element.458.refs_2_, ...), custom_call_target="tpu_custom_call" | custom-call | flops 38999998464 | bytes 113100000 | tf_op jit(solution)/shard_map/cond/branch_1_fun/terms/pallas_call | solution.py:554
  266.4 2.8 advance.57
  269.7 3.0 advance.58
  272.7 15.1 %collective-permute-done.28.came_go.came_stay = bf16[8,384,384]{2,1,0:T(8,128)(2,1)} collective-permute-done((bf16[8,384,384]{2,1,0:T(8,128)(2,1)}, bf16[8,384,384]{2,1,0:T(8,128)(2,1)}, u32[]{:S(2)}, u32[]{:S(2)}) %collective-permute-start.28) | collective-permute-done | bytes 2359328 | tf_op jit(solution)/shard_map/cond/branch_1_fun/ppermute | solution.py:570
  288.3 5.1 %advance.59 = (bf16[4,384,384]{2,1,0:T(8,128)(2,1)S(1)}, bf16[4,384,384]{2,1,0:T(8,128)(2,1)S(1)}) custom-call(s32[4]{0:T(128)S(1)} %copy-done.29, bf16[8,384,384]{2,1,0:T(8,128)(2,1)S(1)} %copy-done.2, bf16[8,384,384]{2,1,0:T(8,128)(2,1)} %collective-permute-done.28.came_go.came_stay, bf16[8,384,384]{2,1,0:T(8,128)(2,1)S(1)} %copy-done.2, ...), custom_call_target="tpu_custom_call" | custom-call | flops 8999999488 | bytes 26100000 | tf_op jit(solution)/shard_map/cond/branch_1_fun/advance/pallas_call | solution.py:589
  298.6 17.0 %collective-permute-done.31.came_go.came_stay = bf16[4,384,384]{2,1,0:T(8,128)(2,1)S(1)} collective-permute-done((bf16[4,384,384]{2,1,0:T(8,128)(2,1)S(1)}, bf16[4,384,384]{2,1,0:T(8,128)(2,1)S(1)}, u32[]{:S(2)}, u32[]{:S(2)}) %collective-permute-start.31) | collective-permute-done | bytes 1179680 | tf_op jit(solution)/shard_map/cond/branch_1_fun/ppermute | solution.py:570
  324.0 3.1 collective-permute-done.36.came_go.came_stay
  331.9 2.8 collective-permute-start.45
  335.8 8.8 %collective-permute-done.34.came_go.came_stay = bf16[2,384,640]{2,1,0:T(8,128)(2,1)S(1)} collective-permute-done((bf16[2,384,640]{2,1,0:T(8,128)(2,1)S(1)}, bf16[2,384,640]{2,1,0:T(8,128)(2,1)S(1)}, u32[]{:S(2)}, u32[]{:S(2)}) %collective-permute-start.34) | collective-permute-done | bytes 983072 | tf_op jit(solution)/shard_map/cond/branch_1_fun/ppermute | solution.py:570
  350.1 9.2 %collective-permute-done.42.came_go.came_stay = bf16[2,208,512]{2,1,0:T(8,128)(2,1)S(1)} collective-permute-done((bf16[2,208,512]{2,1,0:T(8,128)(2,1)S(1)}, bf16[2,208,512]{2,1,0:T(8,128)(2,1)S(1)}, u32[]{:S(2)}, u32[]{:S(2)}) %collective-permute-start.42) | collective-permute-done | bytes 426016 | tf_op jit(solution)/shard_map/cond/branch_1_fun/ppermute | solution.py:570
  363.0 3.4 collective-permute-done.47.refs_3_
  (129 shorter events, 53.5 us)
Async XLA Ops:
  43.4 98.8 %collective-permute-start.49 = (bf16[512,1024]{1,0:T(8,128)(2,1)}, bf16[512,1024]{1,0:T(8,128)(2,1)}, u32[]{:S(2)}, u32[]{:S(2)}) collective-permute-start(bf16[512,1024]{1,0:T(8,128)(2,1)} %get-tuple-element.646), channel_id=1, source_target_pairs={{16,0},{17,1},{18,2},{19,3},{20,4},{21,5},{22,6},{23,7},{24,8},{25... | collective-permute-start | bytes 3145736 | tf_op jit(solution)/shard_map/ppermute | solution.py:793
  157.8 45.5 %collective-permute-start.26 = (bf16[8,256,512]{2,1,0:T(8,128)(2,1)}, bf16[8,256,512]{2,1,0:T(8,128)(2,1)}, u32[]{:S(2)}, u32[]{:S(2)}) collective-permute-start(bf16[8,256,512]{2,1,0:T(8,128)(2,1)} %get-tuple-element.405), channel_id=1, source_target_pairs={{0,1},{1,0},{2,3},{3,2},{4,5},{5,4},{6,7},{7,6},{8,9},{9,8},{10,11... | collective-permute-start | bytes 6291464 | tf_op jit(solution)/shard_map/cond/branch_1_fun/ppermute | solution.py:570
  159.5 52.5 %collective-permute-start.25 = (bf16[8,256,512]{2,1,0:T(8,128)(2,1)}, bf16[8,256,512]{2,1,0:T(8,128)(2,1)}, u32[]{:S(2)}, u32[]{:S(2)}) collective-permute-start(bf16[8,256,512]{2,1,0:T(8,128)(2,1)} %get-tuple-element.407), channel_id=1, source_target_pairs={{0,4},{1,5},{2,6},{3,7},{4,0},{5,1},{6,2},{7,3},{8,12},{9,13},{10,... | collective-permute-start | bytes 6291464 | tf_op jit(solution)/shard_map/cond/branch_1_fun/ppermute | solution.py:570
  201.2 61.2 %collective-permute-start.24 = (bf16[8,384,640]{2,1,0:T(8,128)(2,1)}, bf16[8,384,640]{2,1,0:T(8,128)(2,1)S(1)}, u32[]{:S(2)}, u32[]{:S(2)}) collective-permute-start(bf16[8,384,640]{2,1,0:T(8,128)(2,1)} %get-tuple-element.426), channel_id=1, source_target_pairs={{0,1},{1,0},{2,3},{3,2},{4,5},{5,4},{6,7},{7,6},{8,9},{9,8},{10,11... | collective-permute-start | bytes 11796488 | tf_op jit(solution)/shard_map/cond/branch_1_fun/ppermute | solution.py:570
  201.8 85.9 %collective-permute-start.28 = (bf16[8,384,384]{2,1,0:T(8,128)(2,1)}, bf16[8,384,384]{2,1,0:T(8,128)(2,1)}, u32[]{:S(2)}, u32[]{:S(2)}) collective-permute-start(bf16[8,384,384]{2,1,0:T(8,128)(2,1)} %get-tuple-element.429), channel_id=1, source_target_pairs={{0,1},{1,0},{2,3},{3,2},{4,5},{5,4},{6,7},{7,6},{8,9},{9,8},{10,11... | collective-permute-start | bytes 7077896 | tf_op jit(solution)/shard_map/cond/branch_1_fun/ppermute | solution.py:570
  210.5 54.3 %collective-permute-start.30 = (bf16[4,256,512]{2,1,0:T(8,128)(2,1)}, bf16[4,256,512]{2,1,0:T(8,128)(2,1)}, u32[]{:S(2)}, u32[]{:S(2)}) collective-permute-start(bf16[4,256,512]{2,1,0:T(8,128)(2,1)} %get-tuple-element.433), channel_id=1, source_target_pairs={{0,2},{1,3},{2,0},{3,1},{4,6},{5,7},{6,4},{7,5},{8,10},{9,11},{10,... | collective-permute-start | bytes 3145736 | tf_op jit(solution)/shard_map/cond/branch_1_fun/ppermute | solution.py:570
  219.2 50.0 %collective-permute-start.29 = (bf16[4,256,512]{2,1,0:T(8,128)(2,1)}, bf16[4,256,512]{2,1,0:T(8,128)(2,1)}, u32[]{:S(2)}, u32[]{:S(2)}) collective-permute-start(bf16[4,256,512]{2,1,0:T(8,128)(2,1)} %get-tuple-element.437), channel_id=1, source_target_pairs={{0,8},{1,9},{2,10},{3,11},{4,12},{5,13},{6,14},{7,15},{8,0},{9,1},... | collective-permute-start | bytes 3145736 | tf_op jit(solution)/shard_map/cond/branch_1_fun/ppermute | solution.py:570
  261.8 33.8 %collective-permute-start.32 = (bf16[8,208,512]{2,1,0:T(8,128)(2,1)}, bf16[8,208,512]{2,1,0:T(8,128)(2,1)S(1)}, u32[]{:S(2)}, u32[]{:S(2)}) collective-permute-start(bf16[8,208,512]{2,1,0:T(8,128)(2,1)} %get-tuple-element.467), channel_id=1, source_target_pairs={{0,2},{1,3},{2,0},{3,1},{4,6},{5,7},{6,4},{7,5},{8,10},{9,11},{10,... | collective-permute-start | bytes 5111816 | tf_op jit(solution)/shard_map/cond/branch_1_fun/ppermute | solution.py:570
  262.4 58.7 %collective-permute-start.37 = (bf16[8,208,512]{2,1,0:T(8,128)(2,1)}, bf16[8,208,512]{2,1,0:T(8,128)(2,1)S(1)}, u32[]{:S(2)}, u32[]{:S(2)}) collective-permute-start(bf16[8,208,512]{2,1,0:T(8,128)(2,1)} %get-tuple-element.465), channel_id=1, source_target_pairs={{0,1},{1,0},{2,3},{3,2},{4,5},{5,4},{6,7},{7,6},{8,9},{9,8},{10,11... | collective-permute-start | bytes 5111816 | tf_op jit(solution)/shard_map/cond/branch_1_fun/ppermute | solution.py:570
  264.8 52.1 %collective-permute-start.27 = (bf16[4,384,640]{2,1,0:T(8,128)(2,1)S(1)}, bf16[4,384,640]{2,1,0:T(8,128)(2,1)S(1)}, u32[]{:S(2)}, u32[]{:S(2)}) collective-permute-start(bf16[4,384,640]{2,1,0:T(8,128)(2,1)S(1)} %get-tuple-element.472), channel_id=1, source_target_pairs={{0,2},{1,3},{2,0},{3,1},{4,6},{5,7},{6,4},{7,5},{8,10},{9,11},{10,... | collective-permute-start | bytes 5898248 | tf_op jit(solution)/shard_map/cond/branch_1_fun/ppermute | solution.py:570
  269.2 24.2 %collective-permute-start.33 = (bf16[2,256,512]{2,1,0:T(8,128)(2,1)S(1)}, bf16[2,256,512]{2,1,0:T(8,128)(2,1)S(1)}, u32[]{:S(2)}, u32[]{:S(2)}) collective-permute-start(bf16[2,256,512]{2,1,0:T(8,128)(2,1)S(1)} %get-tuple-element.475), channel_id=1, source_target_pairs={{0,4},{1,5},{2,6},{3,7},{4,0},{5,1},{6,2},{7,3},{8,12},{9,13},{10,... | collective-permute-start | bytes 1572872 | tf_op jit(solution)/shard_map/cond/branch_1_fun/ppermute | solution.py:570
  287.7 32.6 %collective-permute-start.38 = (bf16[2,256,512]{2,1,0:T(8,128)(2,1)S(1)}, bf16[2,256,512]{2,1,0:T(8,128)(2,1)S(1)}, u32[]{:S(2)}, u32[]{:S(2)}) collective-permute-start(bf16[2,256,512]{2,1,0:T(8,128)(2,1)S(1)} %get-tuple-element.479), channel_id=1, source_target_pairs={{0,2},{1,3},{2,0},{3,1},{4,6},{5,7},{6,4},{7,5},{8,10},{9,11},{10,... | collective-permute-start | bytes 1572872 | tf_op jit(solution)/shard_map/cond/branch_1_fun/ppermute | solution.py:570
  293.4 22.2 %collective-permute-start.31 = (bf16[4,384,384]{2,1,0:T(8,128)(2,1)S(1)}, bf16[4,384,384]{2,1,0:T(8,128)(2,1)S(1)}, u32[]{:S(2)}, u32[]{:S(2)}) collective-permute-start(bf16[4,384,384]{2,1,0:T(8,128)(2,1)S(1)} %get-tuple-element.484), channel_id=1, source_target_pairs={{0,4},{1,5},{2,6},{3,7},{4,0},{5,1},{6,2},{7,3},{8,12},{9,13},{10,... | collective-permute-start | bytes 3538952 | tf_op jit(solution)/shard_map/cond/branch_1_fun/ppermute | solution.py:570
  295.6 36.3 %collective-permute-start.39 = (bf16[1,256,512]{2,1,0:T(8,128)(2,1)S(1)}, bf16[1,256,512]{2,1,0:T(8,128)(2,1)S(1)}, u32[]{:S(2)}, u32[]{:S(2)}) collective-permute-start(bf16[1,256,512]{2,1,0:T(8,128)(2,1)S(1)} %get-tuple-element.487), channel_id=1, source_target_pairs={{0,8},{1,9},{2,10},{3,11},{4,12},{5,13},{6,14},{7,15},{8,0},{9,1},... | collective-permute-start | bytes 786440 | tf_op jit(solution)/shard_map/cond/branch_1_fun/ppermute | solution.py:570
  315.6 14.2 %collective-permute-start.35 = (bf16[4,208,512]{2,1,0:T(8,128)(2,1)S(1)}, bf16[4,208,512]{2,1,0:T(8,128)(2,1)S(1)}, u32[]{:S(2)}, u32[]{:S(2)}) collective-permute-start(bf16[4,208,512]{2,1,0:T(8,128)(2,1)S(1)} %get-tuple-element.491), channel_id=1, source_target_pairs={{0,1},{1,0},{2,3},{3,2},{4,5},{5,4},{6,7},{7,6},{8,9},{9,8},{10,11... | collective-permute-start | bytes 2555912 | tf_op jit(solution)/shard_map/cond/branch_1_fun/ppermute | solution.py:570
  316.9 10.2 %collective-permute-start.36 = (bf16[2,384,384]{2,1,0:T(8,128)(2,1)S(1)}, bf16[2,384,384]{2,1,0:T(8,128)(2,1)S(1)}, u32[]{:S(2)}, u32[]{:S(2)}) collective-permute-start(bf16[2,384,384]{2,1,0:T(8,128)(2,1)S(1)} %get-tuple-element.495), channel_id=1, source_target_pairs={{0,2},{1,3},{2,0},{3,1},{4,6},{5,7},{6,4},{7,5},{8,10},{9,11},{10,... | collective-permute-start | bytes 1769480 | tf_op jit(solution)/shard_map/cond/branch_1_fun/ppermute | solution.py:570
  320.3 24.3 %collective-permute-start.34 = (bf16[2,384,640]{2,1,0:T(8,128)(2,1)S(1)}, bf16[2,384,640]{2,1,0:T(8,128)(2,1)S(1)}, u32[]{:S(2)}, u32[]{:S(2)}) collective-permute-start(bf16[2,384,640]{2,1,0:T(8,128)(2,1)S(1)} %get-tuple-element.500), channel_id=1, source_target_pairs={{0,4},{1,5},{2,6},{3,7},{4,0},{5,1},{6,2},{7,3},{8,12},{9,13},{10,... | collective-permute-start | bytes 2949128 | tf_op jit(solution)/shard_map/cond/branch_1_fun/ppermute | solution.py:570
  321.2 13.6 %collective-permute-start.40 = (bf16[1,256,512]{2,1,0:T(8,128)(2,1)S(1)}, bf16[1,256,512]{2,1,0:T(8,128)(2,1)S(1)}, u32[]{:S(2)}, u32[]{:S(2)}) collective-permute-start(bf16[1,256,512]{2,1,0:T(8,128)(2,1)S(1)} %get-tuple-element.503), channel_id=1, source_target_pairs={{0,1},{1,0},{2,3},{3,2},{4,5},{5,4},{6,7},{7,6},{8,9},{9,8},{10,11... | collective-permute-start | bytes 786440 | tf_op jit(solution)/shard_map/cond/branch_1_fun/ppermute | solution.py:570
  327.1 18.5 %collective-permute-start.41 = (bf16[4,208,512]{2,1,0:T(8,128)(2,1)S(1)}, bf16[4,208,512]{2,1,0:T(8,128)(2,1)S(1)}, u32[]{:S(2)}, u32[]{:S(2)}) collective-permute-start(bf16[4,208,512]{2,1,0:T(8,128)(2,1)S(1)} %get-tuple-element.507), channel_id=1, source_target_pairs={{0,2},{1,3},{2,0},{3,1},{4,6},{5,7},{6,4},{7,5},{8,10},{9,11},{10,... | collective-permute-start | bytes 2555912 | tf_op jit(solution)/shard_map/cond/branch_1_fun/ppermute | solution.py:570
  330.7 18.5 %collective-permute-start.43 = (bf16[2,208,512]{2,1,0:T(8,128)(2,1)S(1)}, bf16[2,208,512]{2,1,0:T(8,128)(2,1)S(1)}, u32[]{:S(2)}, u32[]{:S(2)}) collective-permute-start(bf16[2,208,512]{2,1,0:T(8,128)(2,1)S(1)} %get-tuple-element.515), channel_id=1, source_target_pairs={{0,4},{1,5},{2,6},{3,7},{4,0},{5,1},{6,2},{7,3},{8,12},{9,13},{10,... | collective-permute-start | bytes 1277960 | tf_op jit(solution)/shard_map/cond/branch_1_fun/ppermute | solution.py:570
  331.9 28.4 %collective-permute-start.45 = (bf16[1,384,384]{2,1,0:T(8,128)(2,1)S(1)}, bf16[1,384,384]{2,1,0:T(8,128)(2,1)S(1)}, u32[]{:S(2)}, u32[]{:S(2)}) collective-permute-start(bf16[1,384,384]{2,1,0:T(8,128)(2,1)S(1)} %get-tuple-element.511), channel_id=1, source_target_pairs={{0,8},{1,9},{2,10},{3,11},{4,12},{5,13},{6,14},{7,15},{8,0},{9,1},... | collective-permute-start | bytes 884744 | tf_op jit(solution)/shard_map/cond/branch_1_fun/ppermute | solution.py:570
  345.5 16.4 %collective-permute-start.44 = (bf16[1,384,640]{2,1,0:T(8,128)(2,1)S(1)}, bf16[1,384,640]{2,1,0:T(8,128)(2,1)S(1)}, u32[]{:S(2)}, u32[]{:S(2)}) collective-permute-start(bf16[1,384,640]{2,1,0:T(8,128)(2,1)S(1)} %get-tuple-element.521), channel_id=1, source_target_pairs={{0,8},{1,9},{2,10},{3,11},{4,12},{5,13},{6,14},{7,15},{8,0},{9,1},... | collective-permute-start | bytes 1474568 | tf_op jit(solution)/shard_map/cond/branch_1_fun/ppermute | solution.py:570
  346.4 12.9 %collective-permute-start.42 = (bf16[2,208,512]{2,1,0:T(8,128)(2,1)S(1)}, bf16[2,208,512]{2,1,0:T(8,128)(2,1)S(1)}, u32[]{:S(2)}, u32[]{:S(2)}) collective-permute-start(bf16[2,208,512]{2,1,0:T(8,128)(2,1)S(1)} %get-tuple-element.525), channel_id=1, source_target_pairs={{0,4},{1,5},{2,6},{3,7},{4,0},{5,1},{6,2},{7,3},{8,12},{9,13},{10,... | collective-permute-start | bytes 1277960 | tf_op jit(solution)/shard_map/cond/branch_1_fun/ppermute | solution.py:570
  349.8 16.6 %collective-permute-start.47 = (bf16[1,208,512]{2,1,0:T(8,128)(2,1)S(1)}, bf16[1,208,512]{2,1,0:T(8,128)(2,1)S(1)}, u32[]{:S(2)}, u32[]{:S(2)}) collective-permute-start(bf16[1,208,512]{2,1,0:T(8,128)(2,1)S(1)} %get-tuple-element.528), channel_id=1, source_target_pairs={{0,8},{1,9},{2,10},{3,11},{4,12},{5,13},{6,14},{7,15},{8,0},{9,1},... | collective-permute-start | bytes 638984 | tf_op jit(solution)/shard_map/cond/branch_1_fun/ppermute | solution.py:570
  (33 other events, 405.8 us)
